TPU v7x, 32 devices: a whole 2x2x4 slice. The times are simulated.
32 devices in a mesh: grp: 2 (over core), band: 16 (over z, y, x), lev: 1.
Axes of the slice: x: 2, y: 2, z: 4, core: 2. Of those that a mesh axis runs over, the one named last changes fastest.
Arguments:
- spectral: bfloat16 [64, 64, 256], P(('grp', 'band'), None, 'lev'), may hold values from -6 to 6
- synthesis: bfloat16 [64, 128, 64], P(('grp', 'band')), may hold values from -0.75 to 0.75
- analysis: bfloat16 [64, 64, 128], P(('grp', 'band')), may hold values from -0.5 to 0.5
- interp_weights: bfloat16 [8, 256, 512], replicated, may hold values from -0.25 to 0.25
- tube_source: int32 [8192, 1], replicated, may hold values from 0 to 31; in each aligned block of 256 rows (0 to 255, 256 to 511, ...) at most 16 rows name the same one
- tube_column: int32 [8192], replicated, may hold values from 0 to 47
- weight_ids: int32 [8192], replicated, may hold values from 0 to 7
- tube_state: float32 [4, 8192, 256], P(None, ('grp', 'band'), 'lev'), may hold values from -6 to 6
- collision: float32 [8192, 256], P(('grp', 'band'), 'lev'), may hold values from 0.1 to 2
- end_coupling: float32 [4, 8192], P(None, ('grp', 'band')), may hold values from 0.3 to 0.7
- block_inverse: float32 [4, 256, 256], P(None, 'lev'), may hold values from -0.08 to 1.2
Outputs:
- spectral_new: float32 [64, 64, 256], P(('grp', 'band'), None, 'lev')
- tube_new: float32 [4, 8192, 256], P(None, ('grp', 'band'), 'lev')
Inputs may be any that keep to these rules, and one draw needn't show every extreme that they name: `tube_source`: among the 256 tubes of one device (aligned blocks of tube indices), no value appears more than 16 times, and some value appears exactly 16 times.
All inputs are finite; a program needn't handle non-finite values.
Results may differ from a plain program's by a relative error of at most 0.0049.
Values may be sent and summed in bfloat16 or wider, within the bound.
No kernel may reach another device: no remote copies, remote signals or barrier semaphores. Data moves between devices by JAX's collectives and lax.ppermute only.
A program may use at most 64 MiB of HBM per device.

v0:
```python
import math

import jax
import jax.numpy as jnp
from jax import lax
from jax.sharding import PartitionSpec as P

LON = 192
SWEEPS = 4


def extended(cells, sides, width):
    for axis, dim in sides:
        count = lax.axis_size(axis)
        ends = count - 1
        head = lax.slice_in_dim(cells, 0, width, axis=dim)
        tail = lax.slice_in_dim(cells, cells.shape[dim] - width, cells.shape[dim], axis=dim)
        cells = jnp.concatenate(
            [
                lax.ppermute(tail, axis, [(i, (i + 1) % count) for i in range(ends)]),
                cells,
                lax.ppermute(head, axis, [((i + 1) % count, i) for i in range(ends)]),
            ],
            axis=dim,
        )
    return cells


def fourier_table(wavenumbers, points):
    index_grid = (
        jnp.arange(wavenumbers, dtype=jnp.int32)[:, None]
        * jnp.arange(points, dtype=jnp.int32)[None, :]
        % points
    )
    angles = index_grid.astype(jnp.float32) * (2.0 * math.pi / points)
    return jnp.stack([jnp.cos(angles), -jnp.sin(angles)], axis=1)


def in_groups(kernel, rows, operands):
    group_size = math.gcd(rows, 64)
    shaped = tuple(
        (
            operand.reshape((rows // group_size, group_size) + operand.shape[1:])
            for operand in operands
        )
    )
    result = lax.map(lambda pieces: kernel(*pieces), shaped)
    return result.reshape((rows,) + result.shape[2:])


def on_device(
    spectral,
    synthesis,
    analysis,
    interp_weights,
    tube_source,
    tube_column,
    weight_ids,
    tube_state,
    collision,
    end_coupling,
    block_inverse,
):
    highest = lax.Precision.HIGHEST
    sources = lax.axis_size(("grp", "band"))
    myself = lax.axis_index(("grp", "band"))
    wave_local, latitudes, degrees = synthesis.shape
    wave_total = wave_local * sources
    lat_local = latitudes // sources
    columns = spectral.shape[2]
    fields, tubes, points = tube_state.shape
    matrix_count, seg_points, block_size = interp_weights.shape
    level_local = columns // (2 * fields)
    width_cols = block_size // level_local
    lon_blocks = LON // width_cols
    block_count = lat_local * lon_blocks
    capacity = 2 * tubes // sources
    slot_count = sources * capacity
    empty_value = jnp.zeros((), jnp.bfloat16)
    stacked = interp_weights.reshape(matrix_count * seg_points, block_size)
    matrix_ids = jnp.arange(matrix_count, dtype=jnp.int32)
    fourier = jnp.einsum(
        "mlj,mjc->mlc", synthesis, spectral, preferred_element_type=jnp.float32
    ).astype(jnp.bfloat16)
    fourier = lax.all_to_all(fourier, ("grp", "band"), split_axis=1, concat_axis=0, tiled=True)
    table = fourier_table(wave_total, LON)
    spectra = fourier.astype(jnp.float32).reshape(wave_total, lat_local, level_local, fields, 2)
    grid = (
        jnp.einsum("mlzfr,mro->lfzo", spectra, table, precision=highest) * wave_total ** (-0.5)
    ).astype(jnp.bfloat16)
    blocks = (
        grid.reshape(lat_local, fields, level_local, lon_blocks, width_cols)
        .transpose(0, 3, 1, 2, 4)
        .reshape(block_count, fields, block_size)
    )
    owners = tube_source[:, 0].reshape(sources, tubes)
    columns_of = tube_column.reshape(sources, tubes)
    weights_of = weight_ids.reshape(sources, tubes)
    senders = jnp.arange(sources, dtype=jnp.int32)
    slot_ids = jnp.arange(capacity, dtype=jnp.int32)
    row_ids = jnp.arange(tubes, dtype=jnp.int32)
    onehot = (owners[:, :, None] == senders[None, None, :]).astype(jnp.int32)
    ranks = jnp.sum((jnp.cumsum(onehot, axis=1) - onehot) * onehot, axis=2)
    outgoing = (
        (owners[:, None, :] == myself) & (ranks[:, None, :] == slot_ids[None, :, None])
    ).astype(jnp.int32)
    slot_valid = (jnp.sum(outgoing, axis=2) > 0).reshape(slot_count)
    slot_column = jnp.sum(outgoing * columns_of[:, None, :], axis=2).reshape(slot_count)
    my_owner = lax.dynamic_index_in_dim(owners, myself, 0, keepdims=False)
    my_rank = lax.dynamic_index_in_dim(ranks, myself, 0, keepdims=False)
    my_weight = lax.dynamic_index_in_dim(weights_of, myself, 0, keepdims=False)
    arrival = my_owner * capacity + my_rank
    returning = (
        (my_owner[None, None, :] == senders[:, None, None])
        & (my_rank[None, None, :] == slot_ids[None, :, None])
    ).astype(jnp.int32)
    back_valid = (jnp.sum(returning, axis=2) > 0).reshape(slot_count)
    back_row = jnp.sum(returning * row_ids[None, None, :], axis=2).reshape(slot_count)

    def interpolate(chosen, block_rows):
        group = block_rows.shape[0]
        every = jnp.einsum(
            "ak,bk->ab",
            block_rows.reshape(group * fields, block_size),
            stacked,
            preferred_element_type=jnp.float32,
        )
        every = every.reshape(group, fields, matrix_count, seg_points)
        select = (chosen[:, None] == matrix_ids[None, :]).astype(jnp.float32)
        return jnp.einsum("tfwp,tw->tfp", every, select)

    def spread_back(chosen, drag_rows):
        group = drag_rows.shape[0]
        select = (chosen[:, None] == matrix_ids[None, :]).astype(jnp.bfloat16)
        placed = drag_rows[:, :, None, :] * select[:, None, :, None]
        placed = placed.reshape(group * fields, matrix_count * seg_points)
        return jnp.dot(placed, stacked, preferred_element_type=jnp.float32).reshape(
            group, fields, block_size
        )

    picked = jnp.where(slot_valid[:, None, None], blocks[slot_column], empty_value)
    arrived = lax.all_to_all(picked, ("grp", "band"), split_axis=0, concat_axis=0, tiled=True)
    neutral = (
        in_groups(interpolate, tubes, (my_weight, arrived[arrival]))
        .astype(jnp.bfloat16)
        .transpose(1, 0, 2)
    )

    def solve(vector):
        return jnp.einsum("fpq,ftq->ftp", block_inverse, vector, precision=highest)

    forcing = tube_state + neutral.astype(jnp.float32)
    state = solve(forcing)
    for sweep_index in range(SWEEPS):
        padded = extended(state, (("lev", 2),), 1)
        coupled = forcing.at[:, :, 0].add(end_coupling * padded[:, :, 0])
        coupled = coupled.at[:, :, -1].add(end_coupling * padded[:, :, -1])
        state = solve(coupled)
    drag = (collision[None, :, :] * (state - neutral.astype(jnp.float32))).astype(jnp.bfloat16)
    drag_rows = drag.transpose(1, 0, 2)
    own_terms = in_groups(spread_back, tubes, (my_weight, drag_rows)).astype(jnp.bfloat16)
    sent = jnp.where(back_valid[:, None, None], own_terms[back_row], empty_value)
    contrib = lax.all_to_all(sent, ("grp", "band"), split_axis=0, concat_axis=0, tiled=True)
    selector = (
        (slot_column[None, :] == jnp.arange(block_count, dtype=jnp.int32)[:, None])
        & slot_valid[None, :]
    ).astype(jnp.bfloat16)
    tendency = jnp.dot(
        selector,
        contrib.reshape(slot_count, fields * block_size),
        preferred_element_type=jnp.float32,
    )
    tendency = (
        tendency.reshape(lat_local, lon_blocks, fields, level_local, width_cols)
        .transpose(0, 2, 3, 1, 4)
        .reshape(lat_local, fields, level_local, LON)
    )
    analysed = jnp.einsum("lfzo,mro->mlzfr", tendency, table, precision=highest) * LON ** (-0.5)
    analysed = analysed.reshape(wave_total, lat_local, columns).astype(jnp.bfloat16)
    analysed = lax.all_to_all(analysed, ("grp", "band"), split_axis=0, concat_axis=1, tiled=True)
    update = jnp.einsum("mjl,mlc->mjc", analysis, analysed, preferred_element_type=jnp.float32)
    return (spectral.astype(jnp.float32) + update, state)


def solution(mesh):
    placed = (
        P(("grp", "band"), None, "lev"),
        P(("grp", "band"), None, None),
        P(("grp", "band"), None, None),
        P(),
        P(),
        P(),
        P(),
        P(None, ("grp", "band"), "lev"),
        P(("grp", "band"), "lev"),
        P(None, ("grp", "band")),
        P(None, "lev", None),
    )
    return jax.shard_map(
        on_device,
        mesh=mesh,
        in_specs=placed,
        out_specs=(P(("grp", "band"), None, "lev"), P(None, ("grp", "band"), "lev")),
        check_vma=False,
    )
```

profile of v0, /device:TPU:0, one launch (start us, length us, event | category | flops | bytes accessed | tf_op | source)
XLA Modules:
  0.0 259.1 jit_solution(973871587399345572)
XLA Ops:
  2.6 7.3 %all-to-all-start = ((bf16[2,128,256]{2,0,1:T(2,128)(2,1)}), bf16[2,128,256]{2,0,1:T(2,128)(2,1)S(1)}, u32[]{:S(2)}, u32[]{:S(2)}) async-start(bf16[2,128,256]{2,0,1:T(2,128)(2,1)} %copy.169), calls=%async_computation | async-start | bytes 262144 | tf_op jit(solution)/shard_map/all_to_all | solution.py:85
  12.9 18.4 %reduce-window.6 = s32[32,32,2,128]{3,1,2,0:T(8,128)S(1)} reduce-window(s32[32,32,2,128]{3,1,2,0:T(8,128)S(1)} %fusion.49, s32[]{:T(128)} %copy.296), window={size=1x1x1x128 pad=0_0x0_0x0_0x127_0}, to_apply=%region_0.1 | reduce-window | flops 33292288 | bytes 2097156 | tf_op jit(solution)/shard_map/reduce-window
  38.0 3.3 %copy.170 = bf16[2,32,4,256]{2,3,0,1:T(8,128)(2,1)} copy(bf16[2,32,4,256]{3,0,2,1:T(2,128)(2,1)S(1)} %bitcast.258) | data formatting | bytes 262144 | tf_op jit(solution)/shard_map/all_to_all | solution.py:85
  41.3 10.3 %copy.171 = bf16[64,4,32,4,2]{0,2,4,3,1:T(8,128)(2,1)S(1)} copy(bf16[64,4,32,4,2]{1,4,3,2,0:T(2,128)(2,1)} %bitcast.248) | data formatting | bytes 262144 | tf_op jit(solution)/shard_map/reshape | solution.py:87
  55.0 3.1 %gather_fusion = bf16[512,4,512]{2,1,0:T(4,128)(2,1)S(1)} fusion(bf16[48,4,512]{2,1,0:T(4,128)(2,1)S(1)} %reshape.662, s32[1024]{0:T(1024)} %pad_clamp_fusion.2), kind=kCustom, calls=%fused_computation | custom fusion | bytes 4196352 | tf_op jit(solution)/shard_map/gather | solution.py:141
  58.1 2.8 %broadcast_select_fusion = bf16[512,4,512]{2,1,0:T(4,128)(2,1)} fusion(bf16[512,4,512]{2,1,0:T(4,128)(2,1)S(1)} %gather_fusion, pred[512]{0:T(512)(128)(4,1)S(1)} %copy-done.12), kind=kLoop, calls=%fused_computation.31 | loop fusion | flops 1048576 | bytes 4194816 | tf_op jit(solution)/shard_map/jit(_where)/select_n | solution.py:141
  60.9 6.1 %all-to-all-start.1 = ((bf16[512,4,512]{2,1,0:T(4,128)(2,1)}), bf16[512,4,512]{2,1,0:T(4,128)(2,1)}, u32[]{:S(2)}, u32[]{:S(2)}) async-start(bf16[512,4,512]{2,1,0:T(4,128)(2,1)} %broadcast_select_fusion), calls=%async_computation.1 | async-start | bytes 4194304 | tf_op jit(solution)/shard_map/all_to_all | solution.py:142
  67.7 49.7 %all-to-all-done.1 = bf16[512,4,512]{2,1,0:T(4,128)(2,1)} async-done(((bf16[512,4,512]{2,1,0:T(4,128)(2,1)}), bf16[512,4,512]{2,1,0:T(4,128)(2,1)}, u32[]{:S(2)}, u32[]{:S(2)}) %all-to-all-start.1) | async-done | bytes 2097184 | tf_op jit(solution)/shard_map/all_to_all | solution.py:142
  117.4 3.1 %gather_fusion.1 = bf16[256,4,512]{2,1,0:T(4,128)(2,1)S(1)} fusion(bf16[512,4,512]{2,1,0:T(4,128)(2,1)} %all-to-all-done.1, s32[1024]{0:T(1024)S(1)} %pad_clamp_fusion.1), kind=kCustom, calls=%fused_computation.1 | custom fusion | bytes 2098176 | tf_op jit(solution)/shard_map/gather | solution.py:144
  120.5 16.4 %while.30 = (s32[]{:T(128)}, bf16[4,64,4,256]{3,1,0,2:T(8,128)(2,1)}, bf16[4,64,4,512]{3,2,1,0:T(4,128)(2,1)S(1)}, bf16[2048,512]{1,0:T(8,128)(2,1)}, s32[4,64]{1,0:T(4,128)S(1)}, /*index=5*/s32[]{:T(128)}) while((s32[]{:T(128)}, bf16[4,64,4,256]{3,1,0,2:T(8,128)(2,1)}, bf16[4,64,4,512]{3,2,1,0:T(4,128)(2,1)S(1)}, ...), condition=%wide.region_7.8_spmd.clone, body=%wide.region_6.7_spmd.clone.sunk | while | flops 537920000 | bytes 5638477 | solution.py:47
  128.8 2.3 fusion.112
  152.7 3.9 %fusion.38 = (bf16[256,4,256]{2,0,1:T(8,128)(2,1)S(1)}, f32[4,256,256]{2,1,0:T(8,128)}) fusion(f32[256,256]{1,0:T(8,128)S(1)} %copy-done.4, bf16[4,64,4,256]{3,1,0,2:T(8,128)(2,1)} %get-tuple-element.162, f32[4,256,256]{2,1,0:T(8,128)S(1)} %copy-done, f32[4,256,256]{1,0,2:T(4,128)S(1)} %fusion.69), kind=kOutput, calls=%fused_computation.50 | convolution fusion | flops 806354944 | bytes 4456448 | tf_op jit(solution)/shard_map/fpq,ftq->ftp/dot_general | solution.py:150
  156.6 19.7 %while.31 = (s32[]{:T(128)}, bf16[4,64,4,512]{3,1,0,2:T(8,128)(2,1)}, bf16[4,64,4,256]{3,1,0,2:T(8,128)(2,1)S(1)}, s32[4,64]{1,0:T(4,128)S(1)}, bf16[2048,512]{1,0:T(8,128)(2,1)}, /*index=5*/s32[]{:T(128)}) while((s32[]{:T(128)}, bf16[4,64,4,512]{3,1,0,2:T(8,128)(2,1)}, bf16[4,64,4,256]{3,1,0,2:T(8,128)(2,1)S(1)}, ...), condition=%wide.region_9.10_spmd.clone, body=%wide.region_8.9_spmd.clone.sunk | while | flops 537396224 | bytes 12457349 | solution.py:47
  158.5 3.0 %fusion.120 = bf16[4,64,4,512]{3,1,0,2:T(8,128)(2,1)} fusion(bf16[4,64,4,512]{3,1,0,2:T(8,128)(2,1)} %get-tuple-element.371, s32[]{:T(128)} %get-tuple-element.370, bf16[2048,512]{1,0:T(8,128)(2,1)} %get-tuple-element.380, bf16[64,4,2048]{2,0,1:T(8,128)(2,1)S(1)} %mul.326, bf16[64,2048]{1,0:T(8,128)(2,1)S(1)} %bitcast.251), kind=kOutput, calls=%fused_computation.20.clone.1 | convolution fusion | flops 537395200 | bytes 3932672 | tf_op jit(solution)/shard_map/while/body/eval_jaxpr/dot_general | solution.py:137
  163.4 3.1 %fusion.120 = bf16[4,64,4,512]{3,1,0,2:T(8,128)(2,1)} fusion(bf16[4,64,4,512]{3,1,0,2:T(8,128)(2,1)} %get-tuple-element.371, s32[]{:T(128)} %get-tuple-element.370, bf16[2048,512]{1,0:T(8,128)(2,1)} %get-tuple-element.380, bf16[64,4,2048]{2,0,1:T(8,128)(2,1)S(1)} %mul.326, bf16[64,2048]{1,0:T(8,128)(2,1)S(1)} %bitcast.251), kind=kOutput, calls=%fused_computation.20.clone.1 | convolution fusion | flops 537395200 | bytes 3932672 | tf_op jit(solution)/shard_map/while/body/eval_jaxpr/dot_general | solution.py:137
  168.4 3.1 %fusion.120 = bf16[4,64,4,512]{3,1,0,2:T(8,128)(2,1)} fusion(bf16[4,64,4,512]{3,1,0,2:T(8,128)(2,1)} %get-tuple-element.371, s32[]{:T(128)} %get-tuple-element.370, bf16[2048,512]{1,0:T(8,128)(2,1)} %get-tuple-element.380, bf16[64,4,2048]{2,0,1:T(8,128)(2,1)S(1)} %mul.326, bf16[64,2048]{1,0:T(8,128)(2,1)S(1)} %bitcast.251), kind=kOutput, calls=%fused_computation.20.clone.1 | convolution fusion | flops 537395200 | bytes 3932672 | tf_op jit(solution)/shard_map/while/body/eval_jaxpr/dot_general | solution.py:137
  173.3 3.1 %fusion.120 = bf16[4,64,4,512]{3,1,0,2:T(8,128)(2,1)} fusion(bf16[4,64,4,512]{3,1,0,2:T(8,128)(2,1)} %get-tuple-element.371, s32[]{:T(128)} %get-tuple-element.370, bf16[2048,512]{1,0:T(8,128)(2,1)} %get-tuple-element.380, bf16[64,4,2048]{2,0,1:T(8,128)(2,1)S(1)} %mul.326, bf16[64,2048]{1,0:T(8,128)(2,1)S(1)} %bitcast.251), kind=kOutput, calls=%fused_computation.20.clone.1 | convolution fusion | flops 537395200 | bytes 3932672 | tf_op jit(solution)/shard_map/while/body/eval_jaxpr/dot_general | solution.py:137
  178.4 3.8 %gather_fusion.2 = bf16[512,4,512]{2,1,0:T(4,128)(2,1)} fusion(bf16[256,4,512]{2,1,0:T(4,128)(2,1)S(1)} %copy.193, s32[1024]{0:T(1024)S(1)} %pad_clamp_fusion), kind=kCustom, calls=%fused_computation.2 | custom fusion | bytes 4196352 | tf_op jit(solution)/shard_map/gather | solution.py:162
  182.2 3.9 %broadcast_select_fusion.1 = bf16[512,4,512]{2,1,0:T(4,128)(2,1)} fusion(bf16[512,4,512]{2,1,0:T(4,128)(2,1)} %gather_fusion.2, pred[512]{0:T(512)(128)(4,1)S(1)} %gt.27), kind=kLoop, calls=%fused_computation.32 | loop fusion | flops 1048576 | bytes 4194816 | tf_op jit(solution)/shard_map/jit(_where)/select_n | solution.py:162
  186.1 3.5 %all-to-all-start.2 = ((bf16[512,4,512]{2,1,0:T(4,128)(2,1)}), bf16[512,4,512]{2,1,0:T(4,128)(2,1)}, u32[]{:S(2)}, u32[]{:S(2)}) async-start(bf16[512,4,512]{2,1,0:T(4,128)(2,1)} %broadcast_select_fusion.1), calls=%async_computation.2 | async-start | bytes 4194304 | tf_op jit(solution)/shard_map/all_to_all | solution.py:163
  189.7 50.5 %all-to-all-done.2 = bf16[512,4,512]{2,1,0:T(4,128)(2,1)} async-done(((bf16[512,4,512]{2,1,0:T(4,128)(2,1)}), bf16[512,4,512]{2,1,0:T(4,128)(2,1)}, u32[]{:S(2)}, u32[]{:S(2)}) %all-to-all-start.2) | async-done | bytes 2097184 | tf_op jit(solution)/shard_map/all_to_all | solution.py:163
  240.1 3.0 %copy.194 = bf16[512,4,512]{0,2,1:T(8,128)(2,1)S(1)} copy(bf16[512,4,512]{2,1,0:T(4,128)(2,1)} %all-to-all-done.2) | data formatting | bytes 4194304 | tf_op jit(solution)/shard_map/all_to_all | solution.py:163
  245.4 2.6 %fusion.32 = bf16[64,4,32,4,2]{0,2,3,1,4:T(8,128)(2,1)S(1)} fusion(f32[4,4,32,192,1]{2,3,1,0,4:T(8,128)S(1)} %bitcast.252, f32[64,1,192]{2,0,1:T(8,128)S(1)} %get-tuple-element.282, f32[64,1,192]{2,0,1:T(8,128)S(1)} %get-tuple-element.283), kind=kOutput, calls=%fused_computation.40 | convolution fusion | flops 151150592 | bytes 622592 | tf_op jit(solution)/shard_map/lfzo,mro->mlzfr/dot_general | solution.py:178
  248.5 9.7 %all_to_all.43 = bf16[64,4,256]{2,1,0:T(4,128)(2,1)S(1)} all-to-all(bf16[64,4,256]{2,1,0:T(4,128)(2,1)S(1)} %copy.199), channel_id=1, replica_groups=mesh['grp'=2,'band'=16,'lev'=1] {'grp','band'}, dimensions={0} | all-to-all | bytes 262144 | tf_op jit(solution)/shard_map/all_to_all | solution.py:180
  (195 shorter events, 57.7 us)
Async XLA Ops:
  0.6 140.3 %copy-start = (f32[4,256,256]{2,1,0:T(8,128)S(1)}, f32[4,256,256]{2,1,0:T(8,128)}, u32[]{:S(2)}) copy-start(f32[4,256,256]{2,1,0:T(8,128)} %param.41) | copy-start | bytes 3145732
  2.6 35.4 %all-to-all-start = ((bf16[2,128,256]{2,0,1:T(2,128)(2,1)}), bf16[2,128,256]{2,0,1:T(2,128)(2,1)S(1)}, u32[]{:S(2)}, u32[]{:S(2)}) async-start(bf16[2,128,256]{2,0,1:T(2,128)(2,1)} %copy.169), calls=%async_computation | async-start | bytes 262144 | tf_op jit(solution)/shard_map/all_to_all | solution.py:85
  31.3 3.3 %copy-start.8 = (s32[8192]{0:T(1024)S(1)}, s32[8192]{0:T(1024)}, u32[]{:S(2)}) copy-start(s32[8192]{0:T(1024)} %param.36) | copy-start | bytes 98308
  55.0 3.1 %copy-start.12 = (pred[512]{0:T(512)(128)(4,1)S(1)}, pred[512]{0:T(512)(128)(4,1)}, u32[]{:S(2)}) copy-start(pred[512]{0:T(512)(128)(4,1)} %gt.25) | copy-start | bytes 1540
  60.9 6.2 %copy-start.9 = (s32[8192]{0:T(1024)S(1)}, s32[8192]{0:T(1024)}, u32[]{:S(2)}) copy-start(s32[8192]{0:T(1024)} %param.37) | copy-start | bytes 98308
  60.9 6.3 %copy-start.3 = (f32[4,256,256]{2,1,0:T(8,128)S(1)}, f32[4,256,256]{2,1,0:T(8,128)}, u32[]{:S(2)}) copy-start(f32[4,256,256]{2,1,0:T(8,128)} %param.38) | copy-start | bytes 3145732
  60.9 56.5 %all-to-all-start.1 = ((bf16[512,4,512]{2,1,0:T(4,128)(2,1)}), bf16[512,4,512]{2,1,0:T(4,128)(2,1)}, u32[]{:S(2)}, u32[]{:S(2)}) async-start(bf16[512,4,512]{2,1,0:T(4,128)(2,1)} %broadcast_select_fusion), calls=%async_computation.1 | async-start | bytes 4194304 | tf_op jit(solution)/shard_map/all_to_all | solution.py:142
  142.2 1.9 collective-permute-start
  143.4 0.7 collective-permute-start.1
  145.4 3.5 %copy-start.7 = (s32[32,16]{1,0:T(8,128)S(1)}, s32[32,16]{1,0:T(8,128)}, u32[]{:S(2)}) copy-start(s32[32,16]{1,0:T(8,128)} %get-tuple-element.245) | copy-start | bytes 6148
  145.5 1.3 collective-permute-start.2
  146.1 0.7 collective-permute-start.3
  148.1 3.5 %copy-start.11 = (s32[512,1]{0,1:T(1,128)S(1)}, s32[512,1]{0,1:T(1,128)}, u32[]{:S(2)}) copy-start(s32[512,1]{0,1:T(1,128)} %get-tuple-element.280) | copy-start | bytes 6148
  148.1 4.6 %copy-start.4 = (f32[256,256]{1,0:T(8,128)S(1)}, f32[256,256]{1,0:T(8,128)}, u32[]{:S(2)}) copy-start(f32[256,256]{1,0:T(8,128)} %param.39) | copy-start | bytes 786436
  148.1 1.5 collective-permute-start.4
  149.0 0.7 collective-permute-start.5
  151.0 1.7 collective-permute-start.6
  151.7 0.9 collective-permute-start.7
  163.4 3.1 %copy-start.2 = (bf16[4,64,4,256]{3,1,0,2:T(8,128)(2,1)S(1)}, bf16[4,64,4,256]{3,1,0,2:T(8,128)(2,1)}, u32[]{:S(2)}) copy-start(bf16[4,64,4,256]{3,1,0,2:T(8,128)(2,1)} %copy-done.1) | copy-start | bytes 1572868 | tf_op jit(solution)/shard_map/while
  168.3 3.1 %copy-start.2 = (bf16[4,64,4,256]{3,1,0,2:T(8,128)(2,1)S(1)}, bf16[4,64,4,256]{3,1,0,2:T(8,128)(2,1)}, u32[]{:S(2)}) copy-start(bf16[4,64,4,256]{3,1,0,2:T(8,128)(2,1)} %copy-done.1) | copy-start | bytes 1572868 | tf_op jit(solution)/shard_map/while
  173.3 3.1 %copy-start.2 = (bf16[4,64,4,256]{3,1,0,2:T(8,128)(2,1)S(1)}, bf16[4,64,4,256]{3,1,0,2:T(8,128)(2,1)}, u32[]{:S(2)}) copy-start(bf16[4,64,4,256]{3,1,0,2:T(8,128)(2,1)} %copy-done.1) | copy-start | bytes 1572868 | tf_op jit(solution)/shard_map/while
  186.1 54.1 %all-to-all-start.2 = ((bf16[512,4,512]{2,1,0:T(4,128)(2,1)}), bf16[512,4,512]{2,1,0:T(4,128)(2,1)}, u32[]{:S(2)}, u32[]{:S(2)}) async-start(bf16[512,4,512]{2,1,0:T(4,128)(2,1)} %broadcast_select_fusion.1), calls=%async_computation.2 | async-start | bytes 4194304 | tf_op jit(solution)/shard_map/all_to_all | solution.py:163
  245.4 12.9 %copy-start.5 = (bf16[2,64,256]{2,1,0:T(8,128)(2,1)S(1)}, bf16[2,64,256]{2,1,0:T(8,128)(2,1)}, u32[]{:S(2)}) copy-start(bf16[2,64,256]{2,1,0:T(8,128)(2,1)} %param.31) | copy-start | bytes 196612
  245.4 12.9 %copy-start.10 = (bf16[2,64,128]{2,1,0:T(8,128)(2,1)S(1)}, bf16[2,64,128]{2,1,0:T(8,128)(2,1)}, u32[]{:S(2)}) copy-start(bf16[2,64,128]{2,1,0:T(8,128)(2,1)} %param.33) | copy-start | bytes 98308
  (7 other events, 8.1 us)
where the time goes:
time: 260 us; the launch traced here: 259 us
  waiting for transfers between devices  100 us (38%)
  local copies, waits for them, and re-layouts  49.2 us (19%)
  matrix products  40.5 us (16%)
  other arithmetic  35.3 us (14%)
  starting transfers between devices  22.5 us (9%)
  blocking collectives  9.68 us (4%)
    all_to_all x1, waiting for transfers between devices, on_device(): lax.all_to_all(sent, ('grp', 'band'), split_axis=0, concat_axis=0, tiled=...  50.5 us
    all_to_all x1, waiting for transfers between devices, on_device(): lax.all_to_all(picked, ('grp', 'band'), split_axis=0, concat_axis=0, tile...  49.7 us
    another operation x2, other arithmetic  18.5 us
    dot_general x4, matrix products, spread_back(): jnp.dot(placed, stacked, preferred_element_type=jnp.float32)  12.2 us
    reshape x1, local copies, waits for them, and re-layouts, on_device(): fourier.astype(jnp.float32)  10.3 us
    all_to_all x1, blocking collectives, on_device(): lax.all_to_all(analysed, ('grp', 'band'), split_axis=0, concat_axis=1, ti...  9.68 us
    dot_general x4, matrix products, interpolate(): jnp.einsum('ak,bk->ab', block_rows.reshape(group * fields, block_size), s...  9.36 us
    dot_general x5, matrix products, solve(): return jnp.einsum('fpq,ftq->ftp', block_inverse, vector, precision=highest)  8.9 us
  transfers between devices with their start and end apart: 11, of which 2 were waited for; matrix products, arithmetic and copies ran while one was open for 11% of the time, Pallas kernels for 0%

commit v1 on v0

v1 whole, which is shorter than its diff:
```python
import math

import jax
import jax.numpy as jnp
import numpy as np
from jax import lax
from jax.experimental import pallas as pl
from jax.experimental.pallas import tpu as pltpu
from jax.sharding import PartitionSpec as P

LON = 192
SWEEPS = 4
BF = jnp.bfloat16
F32 = jnp.float32
I32 = jnp.int32


def dot(a, b):
    return jnp.dot(a, b, preferred_element_type=F32)


def dot_nt(a, b):
    return lax.dot_general(a, b, (((1,), (1,)), ((), ())), preferred_element_type=F32)


def split(x):
    high = x.astype(BF)
    return high, (x - high.astype(F32)).astype(BF)


def iota(shape, dim):
    return lax.broadcasted_iota(I32, shape, dim)


def onehot(mask):
    return mask.astype(F32).astype(BF)


class Plan:
    def __init__(self, sources, spectral, synthesis, weights, tube_state):
        self.sources = sources
        self.wave_local, self.latitudes, self.degrees = synthesis
        self.waves = self.wave_local * sources
        self.lat_local = self.latitudes // sources
        self.columns = spectral[2]
        self.fields, self.tubes, self.points = tube_state
        self.matrices, _, self.block = weights
        self.levels = self.columns // (2 * self.fields)
        self.width = self.block // self.levels
        self.lon_blocks = LON // self.width
        self.lon_pad = -(-self.lon_blocks // 16) * 16
        self.capacity = 2 * self.tubes // sources
        self.slots = sources * self.capacity
        self.chunk = self.wave_local * self.lat_local
        self.rows = sources * self.chunk
        self.cells = self.lat_local * self.lon_pad
        self.table = self.matrices * self.cells
        self.values = self.fields * self.points
        self.half = self.fields * self.levels


def column_order(plan, transposed):
    n = plan.columns
    natural, moved = (1, 0) if transposed else (0, 1)
    new = iota((n, n), moved)
    part, rest = new // plan.half, new % plan.half
    field, level = rest // plan.levels, rest % plan.levels
    return onehot((level * plan.fields + field) * 2 + part == iota((n, n), natural))


def regrouped_rows(plan, back):
    n = plan.rows
    new = iota((n, n), 0)
    first = plan.sources if back else plan.wave_local
    outer, rest = new // (first * plan.lat_local), new % (first * plan.lat_local)
    middle, last = rest // plan.lat_local, rest % plan.lat_local
    count = plan.wave_local if back else plan.sources
    return onehot((middle * count + outer) * plan.lat_local + last == iota((n, n), 1))


def fourier_tables(plan):
    wave = np.arange(plan.waves)
    lon = np.arange(LON)
    angle = 2.0 * math.pi * ((wave[:, None] * lon[None, :]) % LON) / LON
    full = np.stack([np.cos(angle), -np.sin(angle)], 0)
    full = full.reshape(2, plan.waves, plan.lon_blocks, plan.width)
    full = np.pad(full, ((0, 0), (0, 0), (0, plan.lon_pad - plan.lon_blocks), (0, 0)))
    forward = full.transpose(3, 2, 0, 1).reshape(plan.width * plan.lon_pad, 2 * plan.waves)
    high = forward.astype(BF)
    low = (forward - high.astype(np.float64)).astype(BF)
    synthesis = np.concatenate([high, low], 1)
    analysis = np.concatenate([high.T, low.T, high.T], 1)
    return jnp.asarray(synthesis), jnp.asarray(analysis)


def exchange(plan, array):
    shaped = array.reshape(plan.sources, array.shape[0] // plan.sources, array.shape[1])
    moved = lax.all_to_all(shaped, ("grp", "band"), split_axis=0, concat_axis=0, tiled=True)
    return moved.reshape(array.shape)


def synthesis_kernel(plan, spectral, synthesis, out):
    order = column_order(plan, False)
    parts = []
    for wave in range(plan.wave_local):
        moved = dot(spectral[wave], order).astype(BF)
        parts.append(dot(synthesis[wave], moved).astype(BF))
    stacked = jnp.concatenate(parts, 0)
    out[...] = dot(regrouped_rows(plan, False), stacked).astype(BF)


def routing_kernel(
    plan, me, owners, columns, weight_of, weights, weights_out, pick, pick_t, seat, seat_t
):
    here = me[0]
    sources, tubes, capacity, slots = plan.sources, plan.tubes, plan.capacity, plan.slots
    k = plan.block
    moved = iota((k, k), 1)
    reorder = onehot(
        (moved % plan.levels) * plan.width + moved // plan.levels == iota((k, k), 0)
    )
    for matrix in range(plan.matrices):
        rows = slice(matrix * plan.points, (matrix + 1) * plan.points)
        weights_out[rows, :] = dot(weights[matrix], reorder).astype(BF)

    mask = owners[...] == here
    before = onehot(iota((tubes, tubes), 0) < iota((tubes, tubes), 1))
    rank = dot(onehot(mask), before)
    rank = jnp.where(mask, rank, -1.0)
    column = columns[...]
    cell = column
    for step in range(1, plan.lat_local):
        late = (column >= step * plan.lon_blocks).astype(I32)
        cell = cell + late * (plan.lon_pad - plan.lon_blocks)
    cell = (cell + 1).astype(F32)
    matrix = weight_of[...].astype(F32)
    repeat = onehot(iota((slots, sources), 0) // capacity == iota((slots, sources), 1))
    rank_all = dot(repeat, rank.astype(BF))
    cell_all = dot(repeat, cell.astype(BF))
    matrix_all = dot(repeat, matrix.astype(BF))
    place = (iota((slots, tubes), 0) % capacity).astype(F32)
    chosen = rank_all == place
    cell_slot = jnp.where(chosen, cell_all, 0.0)
    matrix_slot = jnp.where(chosen, matrix_all, 0.0)
    entry = jnp.sum(cell_slot + matrix_slot * plan.cells, axis=1, keepdims=True)
    pick[...] = onehot(entry.astype(I32) - 1 == iota((slots, plan.table), 1))
    ones = jnp.ones((16, tubes), BF)
    entry_row = dot_nt(ones, cell_slot.astype(BF)) + dot_nt(
        ones, matrix_slot.astype(BF)
    ) * plan.cells
    entry_row = entry_row[0:1, :].astype(I32) - 1
    pick_t[...] = onehot(entry_row == iota((plan.table, slots), 0))

    mine = owners[pl.ds(here, 1), :]
    square = (tubes, tubes)
    down, across = iota(square, 0), iota(square, 1)
    mine_col = jnp.sum(jnp.where(down == across, mine, 0), axis=1, keepdims=True)
    same = mine_col == mine
    rank_row = jnp.sum((same & (down < across)).astype(I32), axis=0, keepdims=True)
    rank_col = jnp.sum((same & (across < down)).astype(I32), axis=1, keepdims=True)
    seat[...] = onehot(mine_col * capacity + rank_col == iota((tubes, slots), 1))
    seat_t[...] = onehot(mine * capacity + rank_row == iota((slots, tubes), 0))


def lane_masks(plan, rows):
    group = iota((rows, plan.half), 1) // plan.levels
    return [group == index for index in range(plan.fields)]


def chosen_lanes(plan, masks, pieces):
    result = pieces[0]
    for index in range(1, plan.fields):
        result = jnp.where(masks[index], pieces[index], result)
    return result


def rolled(plan, array, groups):
    groups = groups % plan.fields
    if groups == 0:
        return array
    return pltpu.roll(array, groups * plan.levels, axis=1)


def neutral_kernel(plan, arrived, table, weights, pick, out, blocks, outcomes):
    order = onehot(
        (iota((plan.rows, plan.rows), 0) % plan.waves) * plan.lat_local
        + iota((plan.rows, plan.rows), 0) // plan.waves
        == iota((plan.rows, plan.rows), 1)
    )
    by_lat = dot(order, arrived[...]).astype(BF)
    stacks = []
    for lat in range(plan.lat_local):
        rows = by_lat[lat * plan.waves : (lat + 1) * plan.waves, :]
        stacks.append(jnp.concatenate([rows[:, : plan.half], rows[:, plan.half :]], 0))
    spectra = jnp.concatenate(stacks, 1)
    spectra = jnp.concatenate([spectra, spectra], 0)
    grid = dot(table[...], spectra) * plan.waves ** (-0.5)
    masks = lane_masks(plan, plan.cells)
    per = plan.fields
    for step in range(plan.width // per):
        pieces = []
        for index in range(per):
            start = (step * per + index) * plan.lon_pad
            rows = grid[start : start + plan.lon_pad, :]
            pieces.append(
                jnp.concatenate(
                    [
                        rows[:, lat * plan.half : (lat + 1) * plan.half]
                        for lat in range(plan.lat_local)
                    ],
                    0,
                )
            )
        for field in range(plan.fields):
            turned = [rolled(plan, pieces[index], index - field) for index in range(per)]
            blocks[
                field * plan.cells : (field + 1) * plan.cells,
                step * plan.half : (step + 1) * plan.half,
            ] = chosen_lanes(plan, masks, turned).astype(BF)
    values = blocks[...]
    for matrix in range(plan.matrices):
        part = weights[matrix * plan.points : (matrix + 1) * plan.points, :]
        found = dot_nt(values, part).astype(BF)
        for field in range(plan.fields):
            outcomes[
                matrix * plan.cells : (matrix + 1) * plan.cells,
                field * plan.points : (field + 1) * plan.points,
            ] = found[field * plan.cells : (field + 1) * plan.cells, :]
    out[...] = dot(pick[...], outcomes[...]).astype(BF)


def tube_kernel(
    plan, arrived, seat, seat_t, tube_state, collision, inverse, state_out, out, drag
):
    neutral = dot(seat[...], arrived[...])
    for field in range(plan.fields):
        lanes = slice(field * plan.points, (field + 1) * plan.points)
        wind = neutral[:, lanes]
        force_high, force_low = split(tube_state[field] + wind)
        inverse_high, inverse_low = split(inverse[field])
        state = dot_nt(force_high, inverse_high) + (
            dot_nt(force_high, inverse_low) + dot_nt(force_low, inverse_high)
        )
        state_out[field] = state
        drag[:, lanes] = (collision[...] * (state - wind)).astype(BF)
    out[...] = dot(seat_t[...], drag[...]).astype(BF)


def tendency_kernel(plan, arrived, table, weights, pick_t, out, sums, spread):
    found = dot(pick_t[...], arrived[...]).astype(BF)
    for matrix in range(plan.matrices):
        for field in range(plan.fields):
            sums[
                field * plan.cells : (field + 1) * plan.cells,
                matrix * plan.points : (matrix + 1) * plan.points,
            ] = found[
                matrix * plan.cells : (matrix + 1) * plan.cells,
                field * plan.points : (field + 1) * plan.points,
            ]
    tendency = dot(sums[...], weights[...])
    masks = lane_masks(plan, plan.cells)
    per = plan.fields
    for step in range(plan.width // per):
        lanes = slice(step * plan.half, (step + 1) * plan.half)
        pieces = [
            tendency[field * plan.cells : (field + 1) * plan.cells, lanes]
            for field in range(plan.fields)
        ]
        for index in range(per):
            turned = [
                rolled(plan, pieces[field], field - index) for field in range(plan.fields)
            ]
            mixed = chosen_lanes(plan, masks, turned)
            start = (step * per + index) * plan.lon_pad
            for lat in range(plan.lat_local):
                spread[
                    start : start + plan.lon_pad, lat * plan.half : (lat + 1) * plan.half
                ] = mixed[lat * plan.lon_pad : (lat + 1) * plan.lon_pad, :]
    high, low = split(spread[...])
    analysed = dot(table[...], jnp.concatenate([high, high, low], 0)) * LON ** (-0.5)
    analysed = analysed.astype(BF)
    stacks = []
    for lat in range(plan.lat_local):
        lanes = analysed[:, lat * plan.half : (lat + 1) * plan.half]
        stacks.append(jnp.concatenate([lanes[: plan.waves], lanes[plan.waves :]], 1))
    stacked = jnp.concatenate(stacks, 0)
    new = iota((plan.rows, plan.rows), 0)
    order = onehot(
        (new % plan.lat_local) * plan.waves + new // plan.lat_local
        == iota((plan.rows, plan.rows), 1)
    )
    out[...] = dot(order, stacked).astype(BF)


def analysis_kernel(plan, arrived, analysis, spectral, out):
    grouped = dot(regrouped_rows(plan, True), arrived[...]).astype(BF)
    natural = dot(grouped, column_order(plan, True)).astype(BF)
    for wave in range(plan.wave_local):
        rows = natural[wave * plan.latitudes : (wave + 1) * plan.latitudes, :]
        out[wave] = spectral[wave].astype(F32) + dot(analysis[wave], rows)


def call(plan, kernel, outs, operands, scratch=(), smem=0, flops=0):
    vmem = pl.BlockSpec(memory_space=pltpu.VMEM)
    in_specs = [
        pl.BlockSpec(memory_space=pltpu.SMEM) if i < smem else vmem for i in range(len(operands))
    ]
    size = sum(math.prod(o.shape) * o.dtype.itemsize for o in operands)
    return pl.pallas_call(
        lambda *refs: kernel(plan, *refs),
        out_shape=[jax.ShapeDtypeStruct(s, d) for s, d in outs],
        in_specs=in_specs,
        out_specs=[vmem] * len(outs),
        scratch_shapes=[pltpu.VMEM(s, d) for s, d in scratch],
        cost_estimate=pl.CostEstimate(flops=flops, bytes_accessed=size, transcendentals=0),
        name=kernel.__name__,
    )(*operands)


def swept(plan, neutral, tube_state, end_coupling, block_inverse):
    highest = lax.Precision.HIGHEST
    count = lax.axis_size("lev")
    wind = neutral.reshape(plan.tubes, plan.fields, plan.points).transpose(1, 0, 2)

    def solve(vector):
        return jnp.einsum("fpq,ftq->ftp", block_inverse, vector, precision=highest)

    forcing = tube_state + wind
    state = solve(forcing)
    for _ in range(SWEEPS):
        from_left = lax.ppermute(state[:, :, -1], "lev", [(i, i + 1) for i in range(count - 1)])
        from_right = lax.ppermute(state[:, :, 0], "lev", [(i + 1, i) for i in range(count - 1)])
        coupled = forcing.at[:, :, 0].add(end_coupling * from_left)
        coupled = coupled.at[:, :, -1].add(end_coupling * from_right)
        state = solve(coupled)
    return state, wind


def on_device(
    spectral,
    synthesis,
    analysis,
    interp_weights,
    tube_source,
    tube_column,
    weight_ids,
    tube_state,
    collision,
    end_coupling,
    block_inverse,
):
    sources = lax.axis_size(("grp", "band"))
    plan = Plan(
        sources, spectral.shape, synthesis.shape, interp_weights.shape, tube_state.shape
    )
    me = lax.axis_index(("grp", "band")).astype(I32).reshape(1)
    by_owner = (sources, plan.tubes)
    forward_table, backward_table = fourier_tables(plan)

    (sent,) = call(
        plan, synthesis_kernel, [((plan.rows, plan.columns), BF)], (spectral, synthesis)
    )
    fourier = exchange(plan, sent)
    weights, pick, pick_t, seat, seat_t = call(
        plan,
        routing_kernel,
        [
            ((plan.matrices * plan.points, plan.block), BF),
            ((plan.slots, plan.table), BF),
            ((plan.table, plan.slots), BF),
            ((plan.tubes, plan.slots), BF),
            ((plan.slots, plan.tubes), BF),
        ],
        (
            me,
            tube_source.reshape(by_owner),
            tube_column.reshape(by_owner),
            weight_ids.reshape(by_owner),
            interp_weights,
        ),
        smem=1,
        flops=1 << 31,
    )
    (sent,) = call(
        plan,
        neutral_kernel,
        [((plan.slots, plan.values), BF)],
        (fourier, forward_table, weights, pick),
        scratch=[
            ((plan.fields * plan.cells, plan.block), BF),
            ((plan.table, plan.values), BF),
        ],
    )
    arrived = exchange(plan, sent)
    if lax.axis_size("lev") == 1:
        state, sent = call(
            plan,
            tube_kernel,
            [(tube_state.shape, F32), ((plan.slots, plan.values), BF)],
            (arrived, seat, seat_t, tube_state, collision, block_inverse),
            scratch=[((plan.tubes, plan.values), BF)],
        )
    else:
        neutral = dot(seat, arrived)
        state, wind = swept(plan, neutral, tube_state, end_coupling, block_inverse)
        drag = (collision[None, :, :] * (state - wind)).astype(BF)
        drag = drag.transpose(1, 0, 2).reshape(plan.tubes, plan.values)
        sent = dot(seat_t, drag).astype(BF)
    contrib = exchange(plan, sent)
    (sent,) = call(
        plan,
        tendency_kernel,
        [((plan.rows, plan.columns), BF)],
        (contrib, backward_table, weights, pick_t),
        scratch=[
            ((plan.fields * plan.cells, plan.matrices * plan.points), BF),
            ((plan.width * plan.lon_pad, plan.lat_local * plan.half), F32),
        ],
    )
    analysed = exchange(plan, sent)
    (spectral_new,) = call(
        plan, analysis_kernel, [(spectral.shape, F32)], (analysed, analysis, spectral)
    )
    return spectral_new, state


def solution(mesh):
    placed = (
        P(("grp", "band"), None, "lev"),
        P(("grp", "band"), None, None),
        P(("grp", "band"), None, None),
        P(),
        P(),
        P(),
        P(),
        P(None, ("grp", "band"), "lev"),
        P(("grp", "band"), "lev"),
        P(None, ("grp", "band")),
        P(None, "lev", None),
    )
    return jax.shard_map(
        on_device,
        mesh=mesh,
        in_specs=placed,
        out_specs=(P(("grp", "band"), None, "lev"), P(None, ("grp", "band"), "lev")),
        check_vma=False,
    )
```

time: 260 us -> 116 us (0.45)
  waiting for transfers between devices: 100 us -> 0.01 us
  blocking collectives: 9.68 us -> 76.6 us
  local copies, waits for them, and re-layouts: 49.2 us -> 6.03 us
  matrix products: 40.5 us -> 0 us
  other arithmetic: 35.3 us -> 1.48 us
  Pallas kernels: 0 us -> 22.8 us
  starting transfers between devices: 22.5 us -> 7.32 us
    all_to_all x3 -> x1, waiting for transfers between devices: 100 us -> 0.01 us  [exchange(): lax.all_to_all(shaped, ('grp', 'band'), split_axis=0, concat_axis=0, tile...]
    all_to_all x1 -> x3, blocking collectives: 9.68 us -> 76.6 us  [exchange(): lax.all_to_all(shaped, ('grp', 'band'), split_axis=0, concat_axis=0, tile...]
    dot_general x22 -> x0, matrix products: 40.5 us -> none  [the longest x4 12.2 us: spread_back(): jnp.dot(placed, stacked, preferred_element_type=jnp.float32)]
    pallas_call x0 -> x6, Pallas kernels: none -> 22.8 us  [call(): pl.pallas_call(lambda *refs: kernel(plan, *refs), out_shape=[jax.ShapeDty...]
    another operation x2 -> x0, other arithmetic: 18.5 us -> none
    gather x3 -> x0, local copies, waits for them, and re-layouts: 10 us -> none  [the longest x1 3.81 us: on_device(): own_terms[back_row]]
    reshape x7 -> x3, local copies, waits for them, and re-layouts: 13.1 us -> 3.38 us  [the longest x1 1.38 us: on_device(): weight_ids.reshape(by_owner)]
    all_to_all x3 -> x1, starting transfers between devices: 16.9 us -> 7.32 us  [exchange(): lax.all_to_all(shaped, ('grp', 'band'), split_axis=0, concat_axis=0, tile...]
  transfers between devices with their start and end apart: 11 -> 1, of which waited for: 2 -> 0; matrix products, arithmetic and copies ran while one was open for 11% -> 5% of each run, Pallas kernels for 0% -> 4%
where the time goes in v1:
time: 116 us; the launch traced here: 115 us
  blocking collectives  76.6 us (66%)
  Pallas kernels  22.8 us (20%)
  starting transfers between devices  7.32 us (6%)
  local copies, waits for them, and re-layouts  6.03 us (5%)
  other arithmetic  1.48 us (1%)
    all_to_all x3, blocking collectives, exchange(): lax.all_to_all(shaped, ('grp', 'band'), split_axis=0, concat_axis=0, tile...  76.6 us
    pallas_call x6, Pallas kernels, call(): pl.pallas_call(lambda *refs: kernel(plan, *refs), out_shape=[jax.ShapeDty...  22.8 us
    all_to_all x1, starting transfers between devices, exchange(): lax.all_to_all(shaped, ('grp', 'band'), split_axis=0, concat_axis=0, tile...  7.32 us
    unnamed x4, local copies, waits for them, and re-layouts  2.66 us
  transfers between devices with their start and end apart: 1, of which 0 were waited for; matrix products, arithmetic and copies ran while one was open for 5% of the time, Pallas kernels for 4%

profile of v1, /device:TPU:0, one launch (start us, length us, event | category | flops | bytes accessed | tf_op | source)
XLA Modules:
  0.0 114.9 jit_solution(867119910756313524)
XLA Ops:
  0.6 1.5 %copy.14.refs_1_ = bf16[2,128,64]{2,1,0:T(8,128)(2,1)} copy(bf16[2,128,64]{1,2,0:T(8,128)(2,1)} %param.14) | data formatting | bytes 65536 | tf_op args[1]
  2.1 2.2 %synthesis_kernel.1 = bf16[256,256]{1,0:T(8,128)(2,1)} custom-call(bf16[2,64,256]{2,1,0:T(8,128)(2,1)} %refs_2_.1, bf16[2,128,64]{2,1,0:T(8,128)(2,1)} %copy.14.refs_1_), custom_call_target="tpu_custom_call" | custom-call | bytes 98304 | tf_op jit(solution)/shard_map/synthesis_kernel/pallas_call | solution.py:309
  4.3 7.3 %all-to-all-start = ((bf16[32,8,256]{2,1,0:T(8,128)(2,1)}), bf16[32,8,256]{2,1,0:T(8,128)(2,1)S(1)}, u32[]{:S(2)}, u32[]{:S(2)}) async-start(bf16[32,8,256]{2,1,0:T(8,128)(2,1)} %bitcast.16), calls=%async_computation | async-start | bytes 262144 | tf_op jit(solution)/shard_map/all_to_all | solution.py:98
  11.6 0.5 broadcast.3
  12.2 1.5 %reduce.3 = s32[8192]{0:T(1024)S(1)} reduce(s32[8192,1]{0,1:T(1,128)} %param.17, s32[]{:T(128)} %broadcast.3), dimensions={1}, to_apply=%param.17.reduce_sub_computation.3 | reduce | bytes 65540 | tf_op args[4]
  13.6 0.6 reshape.43.refs_1_
  14.3 1.4 %reshape.44.refs_2_ = s32[32,256]{1,0:T(8,128)} reshape(s32[8192]{0:T(1024)} %param.18) | data formatting | bytes 65536 | tf_op jit(solution)/shard_map/reshape | solution.py:377
  15.6 1.4 %reshape.45.refs_3_ = s32[32,256]{1,0:T(8,128)} reshape(s32[8192]{0:T(1024)} %param.19) | data formatting | bytes 65536 | tf_op jit(solution)/shard_map/reshape | solution.py:378
  17.0 4.8 %routing_kernel.1 = (bf16[2048,512]{1,0:T(8,128)(2,1)}, bf16[512,512]{1,0:T(8,128)(2,1)}, bf16[512,512]{1,0:T(8,128)(2,1)}, bf16[256,512]{1,0:T(8,128)(2,1)}, bf16[512,256]{1,0:T(8,128)(2,1)}) custom-call(s32[1]{0:T(128)} %bitcast.2.refs_0_, s32[32,256]{1,0:T(8,128)} %reshape.43.refs_1_, s32[32,256]{1,0:T(8,128)} %reshape.44.refs_2_, ...), custom_call_target="tpu_custom_call" | custom-call | flops 2147483648 | bytes 2195460 | tf_op jit(solution)/shard_map/routing_kernel/pallas_call | solution.py:309
  21.9 0.0 all-to-all-done
  21.9 0.0 copy-start
  21.9 0.7 copy-done
  22.5 4.5 %neutral_kernel.1 = bf16[512,1024]{1,0:T(8,128)(2,1)} custom-call(bf16[256,256]{1,0:T(8,128)(2,1)} %bitcast.14, bf16[256,256]{1,0:T(8,128)(2,1)} %constant.15.clone.refs_1_, bf16[2048,512]{1,0:T(8,128)(2,1)} %get-tuple-element.9.refs_2_, bf16[512,512]{1,0:T(8,128)(2,1)} %get-tuple-element.10.refs_3_), custom_call_target="tpu_custom_call" | custom-call | bytes 2883584 | tf_op jit(solution)/shard_map/neutral_kernel/pallas_call | solution.py:309
  27.1 34.0 %all_to_all.20 = bf16[32,16,1024]{2,1,0:T(8,128)(2,1)} all-to-all(bf16[32,16,1024]{2,1,0:T(8,128)(2,1)} %bitcast.12), channel_id=1, replica_groups=mesh['grp'=2,'band'=16,'lev'=1] {'grp','band'}, dimensions={0} | all-to-all | bytes 2097152 | tf_op jit(solution)/shard_map/all_to_all | solution.py:98
  61.0 4.4 %tube_kernel.1 = (f32[4,256,256]{2,1,0:T(8,128)}, bf16[512,1024]{1,0:T(8,128)(2,1)}) custom-call(bf16[512,1024]{1,0:T(8,128)(2,1)} %bitcast.10, bf16[256,512]{1,0:T(8,128)(2,1)} %get-tuple-element.11.refs_1_, bf16[512,256]{1,0:T(8,128)(2,1)} %get-tuple-element.12.refs_2_, f32[4,256,256]{2,1,0:T(8,128)} %refs_3_.1, f32[256,256]{1,0:T(8,128)} %refs_4_.3, ...), custom_call_target="tpu_custom_call" | custom-call | bytes 3932160 | tf_op jit(solution)/shard_map/tube_kernel/pallas_call | solution.py:309
  65.4 31.4 %all_to_all.21 = bf16[32,16,1024]{2,1,0:T(8,128)(2,1)} all-to-all(bf16[32,16,1024]{2,1,0:T(8,128)(2,1)} %bitcast.13), channel_id=1, replica_groups=mesh['grp'=2,'band'=16,'lev'=1] {'grp','band'}, dimensions={0} | all-to-all | bytes 2097152 | tf_op jit(solution)/shard_map/all_to_all | solution.py:98
  96.8 4.8 %tendency_kernel.1 = bf16[256,256]{1,0:T(8,128)(2,1)} custom-call(bf16[512,1024]{1,0:T(8,128)(2,1)} %bitcast.11, bf16[128,768]{1,0:T(8,128)(2,1)} %constant.16.clone.refs_1_, bf16[2048,512]{1,0:T(8,128)(2,1)} %get-tuple-element.9.refs_2_, bf16[512,512]{1,0:T(8,128)(2,1)} %get-tuple-element.14.refs_3_), custom_call_target="tpu_custom_call" | custom-call | bytes 3866624 | tf_op jit(solution)/shard_map/tendency_kernel/pallas_call | solution.py:309
  101.6 11.2 %all_to_all.22 = bf16[32,8,256]{2,1,0:T(8,128)(2,1)} all-to-all(bf16[32,8,256]{2,1,0:T(8,128)(2,1)} %bitcast.15), channel_id=1, replica_groups=mesh['grp'=2,'band'=16,'lev'=1] {'grp','band'}, dimensions={0} | all-to-all | bytes 262144 | tf_op jit(solution)/shard_map/all_to_all | solution.py:98
  112.9 2.1 %analysis_kernel.1 = f32[2,64,256]{2,1,0:T(8,128)} custom-call(bf16[256,256]{1,0:T(8,128)(2,1)} %bitcast.17, bf16[2,64,128]{2,1,0:T(8,128)(2,1)} %refs_1_.4, bf16[2,64,256]{2,1,0:T(8,128)(2,1)} %refs_2_.1), custom_call_target="tpu_custom_call" | custom-call | bytes 229376 | tf_op jit(solution)/shard_map/analysis_kernel/pallas_call | solution.py:309
Async XLA Ops:
  4.3 17.5 %all-to-all-start = ((bf16[32,8,256]{2,1,0:T(8,128)(2,1)}), bf16[32,8,256]{2,1,0:T(8,128)(2,1)S(1)}, u32[]{:S(2)}, u32[]{:S(2)}) async-start(bf16[32,8,256]{2,1,0:T(8,128)(2,1)} %bitcast.16), calls=%async_computation | async-start | bytes 262144 | tf_op jit(solution)/shard_map/all_to_all | solution.py:98
  21.9 0.7 copy-start

commit v2 on v1

v2 whole, which is shorter than its diff:
```python
import math

import jax
import jax.numpy as jnp
import numpy as np
from jax import lax
from jax.experimental import pallas as pl
from jax.experimental.pallas import tpu as pltpu
from jax.sharding import Mesh
from jax.sharding import PartitionSpec as P

LON = 192
SWEEPS = 4
BF = jnp.bfloat16
F32 = jnp.float32
I32 = jnp.int32
ALL = ("grp", "hold", "rest")
GROUP = ("grp", "rest")
VMEM_LIMIT = 24 << 20


def dot(a, b):
    return jnp.dot(a, b, preferred_element_type=F32)


def dot_nt(a, b):
    return lax.dot_general(a, b, (((1,), (1,)), ((), ())), preferred_element_type=F32)


def dot_tn(a, b):
    return lax.dot_general(a, b, (((0,), (0,)), ((), ())), preferred_element_type=F32)


def split(x):
    high = x.astype(BF)
    return high, (x - high.astype(F32)).astype(BF)


def iota(shape, dim):
    return lax.broadcasted_iota(I32, shape, dim)


def onehot(mask):
    return mask.astype(F32).astype(BF)


class Plan:
    def __init__(self, grp, copies, rest, spectral, synthesis, weights, tube_state):
        self.grp, self.copies, self.rest = grp, copies, rest
        self.sources = grp * copies * rest
        self.members = grp * rest
        self.wave_local, self.latitudes, self.degrees = synthesis
        self.waves = self.wave_local * self.sources
        self.lat_local = self.latitudes // self.sources
        self.lat_held = self.lat_local * copies
        self.columns = spectral[2]
        self.fields, self.tubes, self.points = tube_state
        self.matrices, _, self.block = weights
        self.levels = self.columns // (2 * self.fields)
        self.width = self.block // self.levels
        self.lon_blocks = LON // self.width
        self.lon_pad = -(-self.lon_blocks // 16) * 16
        self.capacity = 2 * self.tubes // self.sources
        self.slots = self.sources * self.capacity
        self.slots_held = self.members * self.capacity
        self.rows = self.wave_local * self.latitudes
        self.rows_sent = self.rows * copies
        self.cells = self.lat_local * self.lon_pad
        self.table = self.matrices * self.cells
        self.values = self.fields * self.points
        self.half = self.fields * self.levels


def chosen_rows(origin, count):
    origin = np.asarray(origin).reshape(-1)
    return jnp.asarray((origin[:, None] == np.arange(count)[None, :]).astype(BF))


def column_order(plan):
    natural = np.arange(plan.columns).reshape(plan.levels, plan.fields, 2)
    return chosen_rows(natural.transpose(2, 1, 0), plan.columns).T


def block_order(plan):
    natural = np.arange(plan.block).reshape(plan.levels, plan.width)
    return chosen_rows(natural.T, plan.block).T


def wave_rows(plan):
    p = plan
    index = np.arange(p.rows).reshape(p.wave_local, p.grp, p.copies, p.rest, p.lat_local)
    index = index.transpose(1, 3, 2, 0, 4)[:, None]
    return np.broadcast_to(
        index, (p.grp, p.copies, p.rest, p.copies, p.wave_local, p.lat_local)
    )


def latitude_rows(plan):
    p = plan
    index = np.arange(p.rows_sent).reshape(p.sources, p.copies, p.wave_local, p.lat_local)
    return index.transpose(1, 3, 0, 2)


def inverse_rows(plan):
    p = plan
    index = np.arange(p.rows_sent).reshape(p.copies, p.lat_local, p.sources, p.wave_local)
    return index.transpose(2, 0, 3, 1)


def joined_rows(plan):
    origin = np.ascontiguousarray(wave_rows(plan)).reshape(-1)
    return jnp.asarray((np.arange(plan.rows)[:, None] == origin[None, :]).astype(BF))


def fourier_tables(plan):
    wave = np.arange(plan.waves)
    lon = np.arange(LON)
    angle = 2.0 * math.pi * ((wave[:, None] * lon[None, :]) % LON) / LON
    full = np.stack([np.cos(angle), -np.sin(angle)], 0)
    full = full.reshape(2, plan.waves, plan.lon_blocks, plan.width)
    full = np.pad(full, ((0, 0), (0, 0), (0, plan.lon_pad - plan.lon_blocks), (0, 0)))
    forward = full.transpose(3, 2, 0, 1).reshape(plan.width * plan.lon_pad, 2 * plan.waves)
    high = forward.astype(BF)
    low = (forward - high.astype(np.float64)).astype(BF)
    synthesis = np.concatenate([high, low], 1)
    analysis = np.concatenate([high.T, low.T, high.T], 1)
    return jnp.asarray(synthesis), jnp.asarray(analysis)


def exchange(array, axes, count):
    shaped = array.reshape(count, array.shape[0] // count, array.shape[1])
    moved = lax.all_to_all(shaped, axes, split_axis=0, concat_axis=0, tiled=True)
    return moved.reshape(array.shape)


def synthesis_kernel(plan, spectral, synthesis_t, order, rows, out):
    parts = []
    for wave in range(plan.wave_local):
        moved = dot(spectral[wave], order[...]).astype(BF)
        parts.append(dot_tn(synthesis_t[wave], moved).astype(BF))
    out[...] = dot(rows[...], jnp.concatenate(parts, 0)).astype(BF)


def routing_kernel(
    plan, me, owners, columns, weight_of, weights, reorder, weights_out, pick, pick_t, seat, seat_t
):
    p = plan
    mine_g, mine_h, mine_l = me[0], me[1], me[2]
    tubes, capacity = p.tubes, p.capacity
    halves = owners.shape[0] // p.sources
    lanes = owners.shape[1]
    for matrix in range(p.matrices):
        rows = slice(matrix * p.points, (matrix + 1) * p.points)
        weights_out[rows, :] = dot(weights[matrix], reorder[...]).astype(BF)

    column = columns[...]
    cell = column
    for step in range(1, p.lat_local):
        late = (column >= step * p.lon_blocks).astype(I32)
        cell = cell + late * (p.lon_pad - p.lon_blocks)
    facts = [owners[...], cell + 1, weight_of[...]]
    facts = [fact.astype(F32).astype(BF) for fact in facts]

    def rows_of(fact, device):
        taken = []
        for half in range(halves):
            shape = (device.shape[0], p.sources * halves)
            taken.append(dot(onehot(device * halves + half == iota(shape, 1)), fact))
        return jnp.concatenate(taken, 1)

    member = iota((p.members, 1), 0)
    member_g, member_l = member // p.rest, member % p.rest
    device = (member_g * p.copies + mine_h) * p.rest + member_l
    owner, cell, matrix = [rows_of(fact, device) for fact in facts]
    before = onehot(iota((tubes, tubes), 0) < iota((tubes, tubes), 1))
    repeat = onehot(
        iota((p.slots_held, p.members), 0) // capacity == iota((p.slots_held, p.members), 1)
    )
    cell_all = dot(repeat, cell.astype(BF))
    matrix_all = dot(repeat, matrix.astype(BF))
    place = (iota((p.slots_held, tubes), 0) % capacity).astype(F32)
    ones = jnp.ones((16, tubes), BF)
    for copy in range(p.copies):
        source = ((mine_g * p.copies + copy) * p.rest + mine_l).astype(F32)
        mask = owner == source
        rank = jnp.where(mask, dot(onehot(mask), before), -1.0)
        chosen = dot(repeat, rank.astype(BF)) == place
        cell_slot = jnp.where(chosen, cell_all, 0.0)
        matrix_slot = jnp.where(chosen, matrix_all, 0.0)
        entry = jnp.sum(cell_slot + matrix_slot * p.cells, axis=1, keepdims=True)
        pick[copy] = onehot(entry.astype(I32) - 1 == iota((p.slots_held, p.table), 1))
        row = dot_nt(ones, cell_slot.astype(BF)) + dot_nt(ones, matrix_slot.astype(BF)) * p.cells
        row = row[0:1, :].astype(I32) - 1
        pick_t[copy] = onehot(row == iota((p.table, p.slots_held), 0))

    myself = jnp.zeros((16, 1), I32) + ((mine_g * p.copies + mine_h) * p.rest + mine_l)
    mine = rows_of(facts[0], myself)[0:1, :].astype(I32)
    square = (tubes, tubes)
    down, across = iota(square, 0), iota(square, 1)
    mine_col = jnp.sum(jnp.where(down == across, mine, 0), axis=1, keepdims=True)
    same = mine_col == mine
    rank_row = jnp.sum((same & (down < across)).astype(I32), axis=0, keepdims=True)
    rank_col = jnp.sum((same & (across < down)).astype(I32), axis=1, keepdims=True)

    def slot_of(source, rank):
        outer, inner = source // p.rest, source % p.rest
        g, h = outer // p.copies, outer % p.copies
        return ((g * p.rest + inner) * p.copies + h) * capacity + rank

    seat[...] = onehot(slot_of(mine_col, rank_col) == iota((tubes, p.slots), 1))
    seat_t[...] = onehot(slot_of(mine, rank_row) == iota((p.slots, tubes), 0))


def lane_masks(plan, rows):
    group = iota((rows, plan.half), 1) // plan.levels
    return [group == index for index in range(plan.fields)]


def chosen_lanes(plan, masks, pieces):
    result = pieces[0]
    for index in range(1, plan.fields):
        result = jnp.where(masks[index], pieces[index], result)
    return result


def rolled(plan, array, groups):
    groups = groups % plan.fields
    if groups == 0:
        return array
    return pltpu.roll(array, groups * plan.levels, axis=1)


def neutral_kernel(plan, arrived, rows, table, weights, pick, out, blocks, outcomes):
    p = plan
    by_lat = dot(rows[...], arrived[...]).astype(BF)
    stacks = []
    for lat in range(p.lat_held):
        part = by_lat[lat * p.waves : (lat + 1) * p.waves, :]
        stacks.append(jnp.concatenate([part[:, : p.half], part[:, p.half :]], 0))
    spectra = jnp.concatenate(stacks, 1)
    spectra = jnp.concatenate([spectra, spectra], 0)
    grid = dot(table[...], spectra) * p.waves ** (-0.5)
    masks = lane_masks(p, p.cells)
    per = p.fields
    for copy in range(p.copies):
        lats = range(copy * p.lat_local, (copy + 1) * p.lat_local)
        for step in range(p.width // per):
            pieces = []
            for index in range(per):
                start = (step * per + index) * p.lon_pad
                part = grid[start : start + p.lon_pad, :]
                pieces.append(
                    jnp.concatenate([part[:, lat * p.half : (lat + 1) * p.half] for lat in lats], 0)
                )
            for field in range(p.fields):
                turned = [rolled(p, pieces[index], index - field) for index in range(per)]
                first = (copy * p.fields + field) * p.cells
                blocks[first : first + p.cells, step * p.half : (step + 1) * p.half] = (
                    chosen_lanes(p, masks, turned).astype(BF)
                )
    values = blocks[...]
    for matrix in range(p.matrices):
        part = weights[matrix * p.points : (matrix + 1) * p.points, :]
        found = dot_nt(values, part).astype(BF)
        for copy in range(p.copies):
            for field in range(p.fields):
                first = (copy * p.fields + field) * p.cells
                outcomes[
                    copy,
                    matrix * p.cells : (matrix + 1) * p.cells,
                    field * p.points : (field + 1) * p.points,
                ] = found[first : first + p.cells, :]
    for copy in range(p.copies):
        taken = dot(pick[copy], outcomes[copy]).astype(BF)
        out[:, copy] = taken.reshape(p.members, p.capacity, p.values)


def tube_kernel(
    plan, arrived, seat, seat_t, tube_state, collision, inverse, state_out, out, drag
):
    neutral = dot(seat[...], arrived[...])
    for field in range(plan.fields):
        lanes = slice(field * plan.points, (field + 1) * plan.points)
        wind = neutral[:, lanes]
        force_high, force_low = split(tube_state[field] + wind)
        inverse_high, inverse_low = split(inverse[field])
        state = dot_nt(force_high, inverse_high) + (
            dot_nt(force_high, inverse_low) + dot_nt(force_low, inverse_high)
        )
        state_out[field] = state
        drag[:, lanes] = (collision[...] * (state - wind)).astype(BF)
    out[...] = dot(seat_t[...], drag[...]).astype(BF)


def tendency_kernel(plan, arrived, rows, table, weights, pick_t, out, sums, spread):
    p = plan
    for copy in range(p.copies):
        taken = arrived[:, copy].reshape(p.slots_held, p.values)
        found = dot(pick_t[copy], taken).astype(BF)
        for matrix in range(p.matrices):
            for field in range(p.fields):
                first = (copy * p.fields + field) * p.cells
                sums[
                    first : first + p.cells, matrix * p.points : (matrix + 1) * p.points
                ] = found[
                    matrix * p.cells : (matrix + 1) * p.cells,
                    field * p.points : (field + 1) * p.points,
                ]
    tendency = dot(sums[...], weights[...])
    masks = lane_masks(p, p.cells)
    per = p.fields
    for copy in range(p.copies):
        for step in range(p.width // per):
            pieces = []
            for field in range(p.fields):
                first = (copy * p.fields + field) * p.cells
                pieces.append(
                    tendency[first : first + p.cells, step * p.half : (step + 1) * p.half]
                )
            for index in range(per):
                turned = [rolled(p, pieces[field], field - index) for field in range(p.fields)]
                mixed = chosen_lanes(p, masks, turned)
                start = (step * per + index) * p.lon_pad
                for lat in range(p.lat_local):
                    held = copy * p.lat_local + lat
                    spread[
                        start : start + p.lon_pad, held * p.half : (held + 1) * p.half
                    ] = mixed[lat * p.lon_pad : (lat + 1) * p.lon_pad, :]
    high, low = split(spread[...])
    analysed = dot(table[...], jnp.concatenate([high, high, low], 0)) * LON ** (-0.5)
    analysed = analysed.astype(BF)
    stacks = []
    for lat in range(p.lat_held):
        lanes = analysed[:, lat * p.half : (lat + 1) * p.half]
        stacks.append(jnp.concatenate([lanes[: p.waves], lanes[p.waves :]], 1))
    out[...] = dot(rows[...], jnp.concatenate(stacks, 0)).astype(BF)


def analysis_kernel(plan, arrived, rows, order, analysis, spectral, out):
    joined = dot(rows[...], arrived[...]).astype(BF)
    natural = dot_nt(joined, order[...]).astype(BF)
    for wave in range(plan.wave_local):
        part = natural[wave * plan.latitudes : (wave + 1) * plan.latitudes, :]
        out[wave] = spectral[wave].astype(F32) + dot(analysis[wave], part)


def call(plan, kernel, outs, operands, scratch=(), smem=0, flops=0):
    vmem = pl.BlockSpec(memory_space=pltpu.VMEM)
    in_specs = [
        pl.BlockSpec(memory_space=pltpu.SMEM) if i < smem else vmem for i in range(len(operands))
    ]
    size = sum(math.prod(o.shape) * o.dtype.itemsize for o in operands)
    return pl.pallas_call(
        lambda *refs: kernel(plan, *refs),
        out_shape=[jax.ShapeDtypeStruct(s, d) for s, d in outs],
        in_specs=in_specs,
        out_specs=[vmem] * len(outs),
        scratch_shapes=[pltpu.VMEM(s, d) for s, d in scratch],
        cost_estimate=pl.CostEstimate(flops=flops, bytes_accessed=size, transcendentals=0),
        compiler_params=pltpu.CompilerParams(vmem_limit_bytes=VMEM_LIMIT),
        name=kernel.__name__,
    )(*operands)


def swept(plan, neutral, tube_state, end_coupling, block_inverse):
    highest = lax.Precision.HIGHEST
    count = lax.axis_size("lev")
    wind = neutral.reshape(plan.tubes, plan.fields, plan.points).transpose(1, 0, 2)

    def solve(vector):
        return jnp.einsum("fpq,ftq->ftp", block_inverse, vector, precision=highest)

    forcing = tube_state + wind
    state = solve(forcing)
    for _ in range(SWEEPS):
        from_left = lax.ppermute(state[:, :, -1], "lev", [(i, i + 1) for i in range(count - 1)])
        from_right = lax.ppermute(state[:, :, 0], "lev", [(i + 1, i) for i in range(count - 1)])
        coupled = forcing.at[:, :, 0].add(end_coupling * from_left)
        coupled = coupled.at[:, :, -1].add(end_coupling * from_right)
        state = solve(coupled)
    return state, wind


def on_device(
    spectral,
    synthesis,
    analysis,
    interp_weights,
    tube_source,
    tube_column,
    weight_ids,
    tube_state,
    collision,
    end_coupling,
    block_inverse,
):
    plan = Plan(
        *[lax.axis_size(axis) for axis in ALL],
        spectral.shape,
        synthesis.shape,
        interp_weights.shape,
        tube_state.shape,
    )
    p = plan
    me = jnp.stack([lax.axis_index(axis) for axis in ALL]).astype(I32)
    lanes = math.gcd(p.tubes, 128)
    by_lane = (p.sources * p.tubes // lanes, lanes)
    forward_table, backward_table = fourier_tables(p)
    order = column_order(p)

    (sent,) = call(
        p,
        synthesis_kernel,
        [((p.rows_sent, p.columns), BF)],
        (
            spectral,
            synthesis.transpose(0, 2, 1),
            order,
            chosen_rows(wave_rows(p), p.rows),
        ),
    )
    fourier = exchange(sent, ALL, p.sources)
    weights, pick, pick_t, seat, seat_t = call(
        p,
        routing_kernel,
        [
            ((p.matrices * p.points, p.block), BF),
            ((p.copies, p.slots_held, p.table), BF),
            ((p.copies, p.table, p.slots_held), BF),
            ((p.tubes, p.slots), BF),
            ((p.slots, p.tubes), BF),
        ],
        (
            me,
            tube_source.reshape(by_lane),
            tube_column.reshape(by_lane),
            weight_ids.reshape(by_lane),
            interp_weights,
            block_order(p),
        ),
        smem=1,
        flops=1 << 31,
    )
    by_slot = (p.members, p.copies, p.capacity, p.values)
    flat = (p.slots, p.values)
    (sent,) = call(
        p,
        neutral_kernel,
        [(by_slot, BF)],
        (fourier, chosen_rows(latitude_rows(p), p.rows_sent), forward_table, weights, pick),
        scratch=[
            ((p.copies * p.fields * p.cells, p.block), BF),
            ((p.copies, p.table, p.values), BF),
        ],
    )
    arrived = exchange(sent.reshape(flat), GROUP, p.members)
    if lax.axis_size("lev") == 1:
        state, sent = call(
            p,
            tube_kernel,
            [(tube_state.shape, F32), (flat, BF)],
            (arrived, seat, seat_t, tube_state, collision, block_inverse),
            scratch=[((p.tubes, p.values), BF)],
        )
    else:
        state, wind = swept(p, dot(seat, arrived), tube_state, end_coupling, block_inverse)
        drag = (collision[None, :, :] * (state - wind)).astype(BF)
        drag = drag.transpose(1, 0, 2).reshape(p.tubes, p.values)
        sent = dot(seat_t, drag).astype(BF)
    contrib = exchange(sent, GROUP, p.members)
    (sent,) = call(
        p,
        tendency_kernel,
        [((p.rows_sent, p.columns), BF)],
        (
            contrib.reshape(by_slot),
            chosen_rows(inverse_rows(p), p.rows_sent),
            backward_table,
            weights,
            pick_t,
        ),
        scratch=[
            ((p.copies * p.fields * p.cells, p.matrices * p.points), BF),
            ((p.width * p.lon_pad, p.lat_held * p.half), F32),
        ],
    )
    analysed = exchange(sent, ALL, p.sources)
    (spectral_new,) = call(
        p,
        analysis_kernel,
        [(spectral.shape, F32)],
        (analysed, joined_rows(p), order, analysis, spectral),
    )
    return spectral_new, state


def solution(mesh):
    grp, band, lev = (mesh.shape[axis] for axis in ("grp", "band", "lev"))
    copies = 2 if band % 2 == 0 else 1
    parts = mesh.devices.reshape(grp, copies, band // copies, lev)
    mesh = Mesh(parts, ("grp", "hold", "rest", "lev"))
    placed = (
        P(ALL, None, "lev"),
        P(ALL, None, None),
        P(ALL, None, None),
        P(),
        P(),
        P(),
        P(),
        P(None, ALL, "lev"),
        P(ALL, "lev"),
        P(None, ALL),
        P(None, "lev", None),
    )
    return jax.shard_map(
        on_device,
        mesh=mesh,
        in_specs=placed,
        out_specs=(P(ALL, None, "lev"), P(None, ALL, "lev")),
        check_vma=False,
    )
```

time: 116 us -> 87.5 us (0.75)
  blocking collectives: 76.6 us -> 52.8 us
  Pallas kernels: 22.8 us -> 13.5 us
  local copies, waits for them, and re-layouts: 6.03 us -> 11.7 us
  other arithmetic: 1.48 us -> 0.08 us
    all_to_all x3, blocking collectives: 76.6 us -> 52.8 us  [exchange(): lax.all_to_all(shaped, axes, split_axis=0, concat_axis=0, tiled=True)]
    pallas_call x6, Pallas kernels: 22.8 us -> 13.5 us  [call(): pl.pallas_call(lambda *refs: kernel(plan, *refs), out_shape=[jax.ShapeDty...]
    unnamed x4 -> x52, local copies, waits for them, and re-layouts: 2.66 us -> 11.7 us
    reshape x3 -> x0, local copies, waits for them, and re-layouts: 3.38 us -> none  [the longest x1 1.38 us: on_device(): weight_ids.reshape(by_owner)]
    unnamed x1 -> x0, other arithmetic: 1.48 us -> none
  transfers between devices with their start and end apart: 1 -> 1, of which waited for: 0 -> 1; matrix products, arithmetic and copies ran while one was open for 5% -> 0% of each run, Pallas kernels for 4% -> 4%
where the time goes in v2:
time: 87.5 us; the launch traced here: 86.7 us
  blocking collectives  52.8 us (60%)
  Pallas kernels  13.5 us (15%)
  local copies, waits for them, and re-layouts  11.7 us (13%)
  starting transfers between devices  7.33 us (8%)
    all_to_all x3, blocking collectives, exchange(): lax.all_to_all(shaped, axes, split_axis=0, concat_axis=0, tiled=True)  52.8 us
    pallas_call x6, Pallas kernels, call(): pl.pallas_call(lambda *refs: kernel(plan, *refs), out_shape=[jax.ShapeDty...  13.5 us
    unnamed x52, local copies, waits for them, and re-layouts  11.7 us
    all_to_all x1, starting transfers between devices, exchange(): lax.all_to_all(shaped, axes, split_axis=0, concat_axis=0, tiled=True)  7.33 us
  transfers between devices with their start and end apart: 1, of which 1 were waited for; matrix products, arithmetic and copies ran while one was open for 0% of the time, Pallas kernels for 4%

profile of v2, /device:TPU:0, one launch (start us, length us, event | category | flops | bytes accessed | tf_op | source)
XLA Modules:
  0.0 86.7 jit_solution(15073754681368938246)
XLA Ops:
  0.6 0.9 %copy-done.6 = bf16[256,256]{1,0:T(8,128)(2,1)S(1)} copy-done((bf16[256,256]{1,0:T(8,128)(2,1)S(1)}, bf16[256,256]{1,0:T(8,128)(2,1)}, u32[]{:S(2)}) %copy-start.6) | copy-done | bytes 131096
  1.5 0.9 %copy-done.9 = bf16[512,256]{1,0:T(8,128)(2,1)S(1)} copy-done((bf16[512,256]{1,0:T(8,128)(2,1)S(1)}, bf16[512,256]{1,0:T(8,128)(2,1)}, u32[]{:S(2)}) %copy-start.9) | copy-done | bytes 262168
  2.5 0.8 copy-done.10
  3.3 0.8 copy-done.20
  4.1 1.4 %synthesis_kernel.1 = bf16[512,256]{1,0:T(8,128)(2,1)} custom-call(bf16[2,64,256]{2,1,0:T(8,128)(2,1)S(1)} %copy-done.10, bf16[2,64,128]{2,1,0:T(8,128)(2,1)S(1)} %bitcast.22, bf16[256,256]{1,0:T(8,128)(2,1)S(1)} %copy-done.6, bf16[512,256]{1,0:T(8,128)(2,1)S(1)} %copy-done.9), custom_call_target="tpu_custom_call" | custom-call | bytes 491520 | tf_op jit(solution)/shard_map/synthesis_kernel/pallas_call | solution.py:353
  5.5 7.3 %all-to-all-start = ((bf16[32,16,256]{2,1,0:T(8,128)(2,1)}), bf16[32,16,256]{2,1,0:T(8,128)(2,1)S(1)}, u32[]{:S(2)}, u32[]{:S(2)}) async-start(bf16[32,16,256]{2,1,0:T(8,128)(2,1)} %bitcast.1), calls=%async_computation | async-start | bytes 524288 | tf_op jit(solution)/shard_map/all_to_all | solution.py:132
  12.9 1.6 %copy-done.21 = bf16[8,256,512]{2,1,0:T(8,128)(2,1)S(1)} copy-done((bf16[8,256,512]{2,1,0:T(8,128)(2,1)S(1)}, bf16[8,256,512]{2,1,0:T(8,128)(2,1)}, u32[]{:S(2)}) %copy-start.21) | copy-done | bytes 2097176
  14.5 0.8 copy-done.22
  15.2 0.8 copy-done.23
  16.0 0.8 copy-done.24
  16.8 1.0 %copy-done.25 = bf16[512,512]{1,0:T(8,128)(2,1)S(1)} copy-done((bf16[512,512]{1,0:T(8,128)(2,1)S(1)}, bf16[512,512]{1,0:T(8,128)(2,1)}, u32[]{:S(2)}) %copy-start.25) | copy-done | bytes 524312
  17.8 3.4 %routing_kernel.1 = (bf16[2048,512]{1,0:T(8,128)(2,1)S(1)}, bf16[2,256,512]{2,1,0:T(8,128)(2,1)S(1)}, bf16[2,512,256]{2,1,0:T(8,128)(2,1)S(1)}, bf16[256,512]{1,0:T(8,128)(2,1)S(1)}, bf16[512,256]{1,0:T(8,128)(2,1)S(1)}) custom-call(s32[3]{0:T(128)S(1)} %pad_add_fusion.refs_0_, s32[64,128]{1,0:T(8,128)S(1)} %bitcast.23, s32[64,128]{1,0:T(8,128)S(1)} %bitcast.24, ...), custom_call_target="tpu_custom_call" | custom-call | flops 2147483648 | bytes 2719756 | tf_op jit(solution)/shard_map/routing_kernel/pallas_call | solution.py:353
  21.2 0.8 copy-done.4
  22.0 0.7 copy-done.13
  22.7 0.7 copy-done.15
  23.4 0.6 all-to-all-done
  24.0 1.0 %copy-done.5 = bf16[2,256,512]{2,1,0:T(8,128)(2,1)S(1)} copy-done((bf16[2,256,512]{2,1,0:T(8,128)(2,1)S(1)}, bf16[2,256,512]{2,1,0:T(8,128)(2,1)}, u32[]{:S(2)}) %copy-start.5) | copy-done | bytes 524312
  25.0 2.5 %neutral_kernel.1 = bf16[16,2,16,1024]{3,2,1,0:T(8,128)(2,1)S(1)} custom-call(bf16[512,256]{1,0:T(8,128)(2,1)S(1)} %bitcast.18, bf16[512,512]{1,0:T(8,128)(2,1)S(1)} %copy-done.3, bf16[256,256]{1,0:T(8,128)(2,1)S(1)} %copy-done.18, bf16[2048,512]{1,0:T(8,128)(2,1)S(1)} %get-tuple-element.9.refs_3_, bf16[2,256,512]{2,1,0:T(8,128)(2,1)S(1)} %copy-done.5), custom_call_target="tpu_custom_call" | custom-call | bytes 3538944 | tf_op jit(solution)/shard_map/neutral_kernel/pallas_call | solution.py:353
  27.6 19.8 %all_to_all.20 = bf16[16,32,1024]{2,1,0:T(8,128)(2,1)S(1)} all-to-all(bf16[16,32,1024]{2,1,0:T(8,128)(2,1)S(1)} %bitcast.17), channel_id=1, replica_groups=mesh['grp'=2,'hold'=2,'rest'=8,'lev'=1] {'grp','rest'}, dimensions={0} | all-to-all | bytes 2097152 | tf_op jit(solution)/shard_map/all_to_all | solution.py:132
  47.5 1.9 %tube_kernel.1 = (f32[4,256,256]{2,1,0:T(8,128)}, bf16[512,1024]{1,0:T(8,128)(2,1)S(1)}) custom-call(bf16[512,1024]{1,0:T(8,128)(2,1)S(1)} %bitcast.16, bf16[256,512]{1,0:T(8,128)(2,1)S(1)} %copy-done.14, bf16[512,256]{1,0:T(8,128)(2,1)S(1)} %copy-done.16, f32[4,256,256]{2,1,0:T(8,128)S(1)} %copy-done, f32[256,256]{1,0:T(8,128)S(1)} %copy-done.12, ...), custom_call_target="tpu_custom_call" | custom-call | bytes 3932160 | tf_op jit(solution)/shard_map/tube_kernel/pallas_call | solution.py:353
  49.4 18.2 %all_to_all.21 = bf16[16,32,1024]{2,1,0:T(8,128)(2,1)S(1)} all-to-all(bf16[16,32,1024]{2,1,0:T(8,128)(2,1)S(1)} %bitcast.21), channel_id=1, replica_groups=mesh['grp'=2,'hold'=2,'rest'=8,'lev'=1] {'grp','rest'}, dimensions={0} | all-to-all | bytes 2097152 | tf_op jit(solution)/shard_map/all_to_all | solution.py:132
  67.6 3.1 %tendency_kernel.1 = bf16[512,256]{1,0:T(8,128)(2,1)S(1)} custom-call(bf16[16,2,16,1024]{3,2,1,0:T(8,128)(2,1)S(1)} %bitcast.15, bf16[512,512]{1,0:T(8,128)(2,1)S(1)} %copy-done.2, bf16[128,768]{1,0:T(8,128)(2,1)S(1)} %copy-done.17, bf16[2048,512]{1,0:T(8,128)(2,1)S(1)} %get-tuple-element.9.refs_3_, bf16[2,512,256]{2,1,0:T(8,128)(2,1)S(1)} %get-tuple-element.14.refs_4_), custom_call_target="tpu_custom_call" | custom-call | bytes 4390912 | tf_op jit(solution)/shard_map/tendency_kernel/pallas_call | solution.py:353
  70.7 14.8 %all_to_all.22 = bf16[32,16,256]{2,1,0:T(8,128)(2,1)S(1)} all-to-all(bf16[32,16,256]{2,1,0:T(8,128)(2,1)S(1)} %bitcast.19), channel_id=1, replica_groups=mesh['grp'=2,'hold'=2,'rest'=8,'lev'=1] {'grp','hold','rest'}, dimensions={0} | all-to-all | bytes 524288 | tf_op jit(solution)/shard_map/all_to_all | solution.py:132
  85.5 1.2 %analysis_kernel.1 = f32[2,64,256]{2,1,0:T(8,128)} custom-call(bf16[512,256]{1,0:T(8,128)(2,1)S(1)} %bitcast.20, bf16[256,512]{1,0:T(8,128)(2,1)S(1)} %copy-done.8, bf16[256,256]{1,0:T(8,128)(2,1)S(1)} %copy-done.7, bf16[2,64,128]{2,1,0:T(8,128)(2,1)S(1)} %copy-done.19, bf16[2,64,256]{2,1,0:T(8,128)(2,1)S(1)} %copy-done.11), custom_call_target="tpu_custom_call" | custom-call | bytes 753664 | tf_op jit(solution)/shard_map/analysis_kernel/pallas_call | solution.py:353
  (40 shorter events, 0.2 us)
Async XLA Ops:
  0.6 0.9 %copy-start.6 = (bf16[256,256]{1,0:T(8,128)(2,1)S(1)}, bf16[256,256]{1,0:T(8,128)(2,1)}, u32[]{:S(2)}) copy-start(bf16[256,256]{1,0:T(8,128)(2,1)} %constant.40.refs_2_) | copy-start | bytes 393220
  1.5 0.9 %copy-start.9 = (bf16[512,256]{1,0:T(8,128)(2,1)S(1)}, bf16[512,256]{1,0:T(8,128)(2,1)}, u32[]{:S(2)}) copy-start(bf16[512,256]{1,0:T(8,128)(2,1)} %constant.32.clone.refs_3_) | copy-start | bytes 786436
  2.5 0.8 copy-start.10
  3.3 0.8 copy-start.20
  5.5 18.5 %all-to-all-start = ((bf16[32,16,256]{2,1,0:T(8,128)(2,1)}), bf16[32,16,256]{2,1,0:T(8,128)(2,1)S(1)}, u32[]{:S(2)}, u32[]{:S(2)}) async-start(bf16[32,16,256]{2,1,0:T(8,128)(2,1)} %bitcast.1), calls=%async_computation | async-start | bytes 524288 | tf_op jit(solution)/shard_map/all_to_all | solution.py:132
  12.9 1.6 %copy-start.21 = (bf16[8,256,512]{2,1,0:T(8,128)(2,1)S(1)}, bf16[8,256,512]{2,1,0:T(8,128)(2,1)}, u32[]{:S(2)}) copy-start(bf16[8,256,512]{2,1,0:T(8,128)(2,1)} %refs_4_.3) | copy-start | bytes 6291460
  14.5 0.8 copy-start.22
  15.2 0.8 copy-start.23
  16.8 1.0 %copy-start.25 = (bf16[512,512]{1,0:T(8,128)(2,1)S(1)}, bf16[512,512]{1,0:T(8,128)(2,1)}, u32[]{:S(2)}) copy-start(bf16[512,512]{1,0:T(8,128)(2,1)} %constant.41.refs_5_) | copy-start | bytes 1572868
  17.8 6.2 %copy-start.3 = (bf16[512,512]{1,0:T(8,128)(2,1)S(1)}, bf16[512,512]{1,0:T(8,128)(2,1)}, u32[]{:S(2)}) copy-start(bf16[512,512]{1,0:T(8,128)(2,1)} %constant.34.clone.refs_1_) | copy-start | bytes 1572868
  17.8 6.2 %copy-start.18 = (bf16[256,256]{1,0:T(8,128)(2,1)S(1)}, bf16[256,256]{1,0:T(8,128)(2,1)}, u32[]{:S(2)}) copy-start(bf16[256,256]{1,0:T(8,128)(2,1)} %constant.29.clone.refs_2_) | copy-start | bytes 393220
  21.2 0.8 copy-start.4
  24.0 1.0 %copy-start.5 = (bf16[2,256,512]{2,1,0:T(8,128)(2,1)S(1)}, bf16[2,256,512]{2,1,0:T(8,128)(2,1)}, u32[]{:S(2)}) copy-start(bf16[2,256,512]{2,1,0:T(8,128)(2,1)} %copy-done.4) | copy-start | bytes 1572868
  25.0 22.4 %copy-start.12 = (f32[256,256]{1,0:T(8,128)S(1)}, f32[256,256]{1,0:T(8,128)}, u32[]{:S(2)}) copy-start(f32[256,256]{1,0:T(8,128)} %refs_4_.4) | copy-start | bytes 786436
  25.0 22.4 %copy-start.14 = (bf16[256,512]{1,0:T(8,128)(2,1)S(1)}, bf16[256,512]{1,0:T(8,128)(2,1)}, u32[]{:S(2)}) copy-start(bf16[256,512]{1,0:T(8,128)(2,1)} %copy-done.13) | copy-start | bytes 786436
  25.0 22.4 %copy-start.16 = (bf16[512,256]{1,0:T(8,128)(2,1)S(1)}, bf16[512,256]{1,0:T(8,128)(2,1)}, u32[]{:S(2)}) copy-start(bf16[512,256]{1,0:T(8,128)(2,1)} %copy-done.15) | copy-start | bytes 786436
  27.6 19.9 %copy-start = (f32[4,256,256]{2,1,0:T(8,128)S(1)}, f32[4,256,256]{2,1,0:T(8,128)}, u32[]{:S(2)}) copy-start(f32[4,256,256]{2,1,0:T(8,128)} %refs_3_.3) | copy-start | bytes 3145732
  27.6 19.9 %copy-start.1 = (f32[4,256,256]{2,1,0:T(8,128)S(1)}, f32[4,256,256]{2,1,0:T(8,128)}, u32[]{:S(2)}) copy-start(f32[4,256,256]{2,1,0:T(8,128)} %refs_5_.1) | copy-start | bytes 3145732
  47.5 20.1 %copy-start.2 = (bf16[512,512]{1,0:T(8,128)(2,1)S(1)}, bf16[512,512]{1,0:T(8,128)(2,1)}, u32[]{:S(2)}) copy-start(bf16[512,512]{1,0:T(8,128)(2,1)} %constant.35.clone.refs_1_) | copy-start | bytes 1572868
  47.5 20.1 %copy-start.17 = (bf16[128,768]{1,0:T(8,128)(2,1)S(1)}, bf16[128,768]{1,0:T(8,128)(2,1)}, u32[]{:S(2)}) copy-start(bf16[128,768]{1,0:T(8,128)(2,1)} %constant.30.clone.refs_2_) | copy-start | bytes 589828
  67.6 17.9 %copy-start.7 = (bf16[256,256]{1,0:T(8,128)(2,1)S(1)}, bf16[256,256]{1,0:T(8,128)(2,1)}, u32[]{:S(2)}) copy-start(bf16[256,256]{1,0:T(8,128)(2,1)} %constant.40.refs_2_) | copy-start | bytes 393220
  67.6 17.9 %copy-start.8 = (bf16[256,512]{1,0:T(8,128)(2,1)S(1)}, bf16[256,512]{1,0:T(8,128)(2,1)}, u32[]{:S(2)}) copy-start(bf16[256,512]{1,0:T(8,128)(2,1)} %constant.36.clone.refs_1_) | copy-start | bytes 786436
  67.6 17.9 %copy-start.11 = (bf16[2,64,256]{2,1,0:T(8,128)(2,1)S(1)}, bf16[2,64,256]{2,1,0:T(8,128)(2,1)}, u32[]{:S(2)}) copy-start(bf16[2,64,256]{2,1,0:T(8,128)(2,1)} %refs_4_.5) | copy-start | bytes 196612
  67.6 17.9 %copy-start.19 = (bf16[2,64,128]{2,1,0:T(8,128)(2,1)S(1)}, bf16[2,64,128]{2,1,0:T(8,128)(2,1)}, u32[]{:S(2)}) copy-start(bf16[2,64,128]{2,1,0:T(8,128)(2,1)} %refs_3_.4) | copy-start | bytes 98308
  (3 other events, 2.2 us)

commit v3 on v2

--- a/solution.py
+++ b/solution.py
@@ -89,10 +89,7 @@
 def wave_rows(plan):
     p = plan
     index = np.arange(p.rows).reshape(p.wave_local, p.grp, p.copies, p.rest, p.lat_local)
-    index = index.transpose(1, 3, 2, 0, 4)[:, None]
-    return np.broadcast_to(
-        index, (p.grp, p.copies, p.rest, p.copies, p.wave_local, p.lat_local)
-    )
+    return index.transpose(1, 3, 2, 0, 4)
 
 
 def latitude_rows(plan):
@@ -105,11 +102,6 @@
     p = plan
     index = np.arange(p.rows_sent).reshape(p.copies, p.lat_local, p.sources, p.wave_local)
     return index.transpose(2, 0, 3, 1)
-
-
-def joined_rows(plan):
-    origin = np.ascontiguousarray(wave_rows(plan)).reshape(-1)
-    return jnp.asarray((np.arange(plan.rows)[:, None] == origin[None, :]).astype(BF))
 
 
 def fourier_tables(plan):
@@ -133,26 +125,37 @@
     return moved.reshape(array.shape)
 
 
-def synthesis_kernel(plan, spectral, synthesis_t, order, rows, out):
-    parts = []
-    for wave in range(plan.wave_local):
+def synthesis_kernel(plan, wait, spectral, synthesis_t, order, rows, out):
+    p = plan
+    total = 0.0
+    for wave in range(p.wave_local):
         moved = dot(spectral[wave], order[...]).astype(BF)
-        parts.append(dot_tn(synthesis_t[wave], moved).astype(BF))
-    out[...] = dot(rows[...], jnp.concatenate(parts, 0)).astype(BF)
+        here = rows[:, wave * p.latitudes : (wave + 1) * p.latitudes]
+        placed = dot_nt(here, synthesis_t[wave]).astype(BF)
+        total = total + dot(placed, moved)
+    moved = total.astype(BF).reshape(p.grp, p.rows // p.grp, p.columns)
+    for copy in range(p.copies):
+        out[:, copy] = moved
 
 
 def routing_kernel(
-    plan, me, owners, columns, weight_of, weights, reorder, weights_out, pick, pick_t, seat, seat_t
+    plan,
+    wait,
+    me,
+    owners,
+    columns,
+    weight_of,
+    weights,
+    reorder,
+    weights_out,
+    pick_t,
+    seat_t,
 ):
     p = plan
     mine_g, mine_h, mine_l = me[0], me[1], me[2]
     tubes, capacity = p.tubes, p.capacity
     halves = owners.shape[0] // p.sources
     lanes = owners.shape[1]
-    for matrix in range(p.matrices):
-        rows = slice(matrix * p.points, (matrix + 1) * p.points)
-        weights_out[rows, :] = dot(weights[matrix], reorder[...]).astype(BF)
-
     column = columns[...]
     cell = column
     for step in range(1, p.lat_local):
@@ -187,8 +190,6 @@
         chosen = dot(repeat, rank.astype(BF)) == place
         cell_slot = jnp.where(chosen, cell_all, 0.0)
         matrix_slot = jnp.where(chosen, matrix_all, 0.0)
-        entry = jnp.sum(cell_slot + matrix_slot * p.cells, axis=1, keepdims=True)
-        pick[copy] = onehot(entry.astype(I32) - 1 == iota((p.slots_held, p.table), 1))
         row = dot_nt(ones, cell_slot.astype(BF)) + dot_nt(ones, matrix_slot.astype(BF)) * p.cells
         row = row[0:1, :].astype(I32) - 1
         pick_t[copy] = onehot(row == iota((p.table, p.slots_held), 0))
@@ -200,15 +201,19 @@
     mine_col = jnp.sum(jnp.where(down == across, mine, 0), axis=1, keepdims=True)
     same = mine_col == mine
     rank_row = jnp.sum((same & (down < across)).astype(I32), axis=0, keepdims=True)
-    rank_col = jnp.sum((same & (across < down)).astype(I32), axis=1, keepdims=True)
 
     def slot_of(source, rank):
         outer, inner = source // p.rest, source % p.rest
         g, h = outer // p.copies, outer % p.copies
         return ((g * p.rest + inner) * p.copies + h) * capacity + rank
 
-    seat[...] = onehot(slot_of(mine_col, rank_col) == iota((tubes, p.slots), 1))
     seat_t[...] = onehot(slot_of(mine, rank_row) == iota((p.slots, tubes), 0))
+
+    wait(5)
+    wait(4)
+    for matrix in range(p.matrices):
+        rows = slice(matrix * p.points, (matrix + 1) * p.points)
+        weights_out[rows, :] = dot(weights[matrix], reorder[...]).astype(BF)
 
 
 def lane_masks(plan, rows):
@@ -230,7 +235,7 @@
     return pltpu.roll(array, groups * plan.levels, axis=1)
 
 
-def neutral_kernel(plan, arrived, rows, table, weights, pick, out, blocks, outcomes):
+def neutral_kernel(plan, wait, arrived, rows, table, weights, pick_t, out, blocks, outcomes):
     p = plan
     by_lat = dot(rows[...], arrived[...]).astype(BF)
     stacks = []
@@ -271,14 +276,15 @@
                     field * p.points : (field + 1) * p.points,
                 ] = found[first : first + p.cells, :]
     for copy in range(p.copies):
-        taken = dot(pick[copy], outcomes[copy]).astype(BF)
+        taken = dot_tn(pick_t[copy], outcomes[copy]).astype(BF)
         out[:, copy] = taken.reshape(p.members, p.capacity, p.values)
 
 
 def tube_kernel(
-    plan, arrived, seat, seat_t, tube_state, collision, inverse, state_out, out, drag
+    plan, wait, arrived, seat_t, tube_state, collision, inverse, state_out, out, drag, held, done
 ):
-    neutral = dot(seat[...], arrived[...])
+    neutral = dot_tn(seat_t[...], arrived[...])
+    copies = []
     for field in range(plan.fields):
         lanes = slice(field * plan.points, (field + 1) * plan.points)
         wind = neutral[:, lanes]
@@ -287,12 +293,18 @@
         state = dot_nt(force_high, inverse_high) + (
             dot_nt(force_high, inverse_low) + dot_nt(force_low, inverse_high)
         )
-        state_out[field] = state
+        held[field] = state
+        copies.append(
+            pltpu.make_async_copy(held.at[field], state_out.at[field], done.at[field])
+        )
+        copies[-1].start()
         drag[:, lanes] = (collision[...] * (state - wind)).astype(BF)
     out[...] = dot(seat_t[...], drag[...]).astype(BF)
-
-
-def tendency_kernel(plan, arrived, rows, table, weights, pick_t, out, sums, spread):
+    for copy in copies:
+        copy.wait()
+
+
+def tendency_kernel(plan, wait, arrived, rows, table, weights, pick_t, out, sums, spread):
     p = plan
     for copy in range(p.copies):
         taken = arrived[:, copy].reshape(p.slots_held, p.values)
@@ -336,26 +348,61 @@
     out[...] = dot(rows[...], jnp.concatenate(stacks, 0)).astype(BF)
 
 
-def analysis_kernel(plan, arrived, rows, order, analysis, spectral, out):
-    joined = dot(rows[...], arrived[...]).astype(BF)
-    natural = dot_nt(joined, order[...]).astype(BF)
+def analysis_kernel(plan, wait, arrived, rows, order, analysis, spectral, out):
+    joined = arrived[:, 0].astype(F32)
+    for copy in range(1, plan.copies):
+        joined = joined + arrived[:, copy].astype(F32)
+    joined = joined.reshape(plan.rows, plan.columns).astype(BF)
+    natural = dot_tn(rows[...], joined).astype(BF)
+    natural = dot_nt(natural, order[...]).astype(BF)
     for wave in range(plan.wave_local):
         part = natural[wave * plan.latitudes : (wave + 1) * plan.latitudes, :]
         out[wave] = spectral[wave].astype(F32) + dot(analysis[wave], part)
 
 
-def call(plan, kernel, outs, operands, scratch=(), smem=0, flops=0):
+def call(
+    plan, kernel, outs, operands, scratch=(), smem=0, fetched=(), late=(), stored=(), flops=0
+):
     vmem = pl.BlockSpec(memory_space=pltpu.VMEM)
+    hbm = pl.BlockSpec(memory_space=pltpu.HBM)
+    scalar = pl.BlockSpec(memory_space=pltpu.SMEM)
     in_specs = [
-        pl.BlockSpec(memory_space=pltpu.SMEM) if i < smem else vmem for i in range(len(operands))
+        scalar if i < smem else hbm if i in fetched else vmem for i in range(len(operands))
     ]
     size = sum(math.prod(o.shape) * o.dtype.itemsize for o in operands)
+    operands = [
+        pltpu.with_memory_space_constraint(o, pltpu.HBM) if i in fetched else o
+        for i, o in enumerate(operands)
+    ]
+    held = [pltpu.VMEM(s, d) for s, d in scratch]
+    for i in stored:
+        held += [pltpu.VMEM(*outs[i]), pltpu.SemaphoreType.DMA(outs[i][0][:1])]
+    if fetched:
+        held += [pltpu.VMEM(operands[i].shape, operands[i].dtype) for i in fetched]
+        held += [pltpu.SemaphoreType.DMA((len(fetched),))]
+
+    def body(*refs):
+        refs = list(refs)
+        copies = {}
+        for place, i in enumerate(fetched):
+            target = refs[place - 1 - len(fetched)]
+            copies[i] = pltpu.make_async_copy(refs[i], target, refs[-1].at[place])
+            copies[i].start()
+        for place, i in enumerate(fetched):
+            refs[i] = refs[place - 1 - len(fetched)]
+        for i in fetched:
+            if i not in late:
+                copies[i].wait()
+        if fetched:
+            refs = refs[: -1 - len(fetched)]
+        kernel(plan, lambda i: copies[i].wait(), *refs)
+
     return pl.pallas_call(
-        lambda *refs: kernel(plan, *refs),
+        body,
         out_shape=[jax.ShapeDtypeStruct(s, d) for s, d in outs],
         in_specs=in_specs,
-        out_specs=[vmem] * len(outs),
-        scratch_shapes=[pltpu.VMEM(s, d) for s, d in scratch],
+        out_specs=[hbm if i in stored else vmem for i in range(len(outs))],
+        scratch_shapes=held,
         cost_estimate=pl.CostEstimate(flops=flops, bytes_accessed=size, transcendentals=0),
         compiler_params=pltpu.CompilerParams(vmem_limit_bytes=VMEM_LIMIT),
         name=kernel.__name__,
@@ -407,27 +454,23 @@
     by_lane = (p.sources * p.tubes // lanes, lanes)
     forward_table, backward_table = fourier_tables(p)
     order = column_order(p)
+    wave_order = chosen_rows(wave_rows(p), p.rows)
 
     (sent,) = call(
         p,
         synthesis_kernel,
-        [((p.rows_sent, p.columns), BF)],
-        (
-            spectral,
-            synthesis.transpose(0, 2, 1),
-            order,
-            chosen_rows(wave_rows(p), p.rows),
-        ),
-    )
-    fourier = exchange(sent, ALL, p.sources)
-    weights, pick, pick_t, seat, seat_t = call(
+        [((p.grp, p.copies, p.rows // p.grp, p.columns), BF)],
+        (spectral, synthesis.transpose(0, 2, 1), order, wave_order),
+        fetched=(0, 1, 2, 3),
+    )
+    flat = (p.rows_sent, p.columns)
+    fourier = exchange(sent.reshape(flat), ALL, p.sources)
+    weights, pick_t, seat_t = call(
         p,
         routing_kernel,
         [
             ((p.matrices * p.points, p.block), BF),
-            ((p.copies, p.slots_held, p.table), BF),
             ((p.copies, p.table, p.slots_held), BF),
-            ((p.tubes, p.slots), BF),
             ((p.slots, p.tubes), BF),
         ],
         (
@@ -439,6 +482,8 @@
             block_order(p),
         ),
         smem=1,
+        fetched=(1, 2, 3, 5, 4),
+        late=(4, 5),
         flops=1 << 31,
     )
     by_slot = (p.members, p.copies, p.capacity, p.values)
@@ -447,7 +492,7 @@
         p,
         neutral_kernel,
         [(by_slot, BF)],
-        (fourier, chosen_rows(latitude_rows(p), p.rows_sent), forward_table, weights, pick),
+        (fourier, chosen_rows(latitude_rows(p), p.rows_sent), forward_table, weights, pick_t),
         scratch=[
             ((p.copies * p.fields * p.cells, p.block), BF),
             ((p.copies, p.table, p.values), BF),
@@ -459,11 +504,12 @@
             p,
             tube_kernel,
             [(tube_state.shape, F32), (flat, BF)],
-            (arrived, seat, seat_t, tube_state, collision, block_inverse),
+            (arrived, seat_t, tube_state, collision, block_inverse),
             scratch=[((p.tubes, p.values), BF)],
+            stored=(0,),
         )
     else:
-        state, wind = swept(p, dot(seat, arrived), tube_state, end_coupling, block_inverse)
+        state, wind = swept(p, dot_tn(seat_t, arrived), tube_state, end_coupling, block_inverse)
         drag = (collision[None, :, :] * (state - wind)).astype(BF)
         drag = drag.transpose(1, 0, 2).reshape(p.tubes, p.values)
         sent = dot(seat_t, drag).astype(BF)
@@ -489,7 +535,13 @@
         p,
         analysis_kernel,
         [(spectral.shape, F32)],
-        (analysed, joined_rows(p), order, analysis, spectral),
+        (
+            analysed.reshape(p.grp, p.copies, p.rows // p.grp, p.columns),
+            wave_order,
+            order,
+            analysis,
+            spectral,
+        ),
     )
     return spectral_new, state
 

time: 87.5 us -> 79.7 us (0.911)
  local copies, waits for them, and re-layouts: 11.7 us -> 0.75 us
  waiting for transfers between devices: 0.56 us -> 6.31 us
  blocking collectives: 52.8 us -> 49.4 us
  Pallas kernels: 13.5 us -> 14.8 us
    unnamed x52 -> x26, local copies, waits for them, and re-layouts: 11.7 us -> 0.75 us
    all_to_all x1, waiting for transfers between devices: 0.56 us -> 6.31 us  [exchange(): lax.all_to_all(shaped, axes, split_axis=0, concat_axis=0, tiled=True)]
    all_to_all x3, blocking collectives: 52.8 us -> 49.4 us  [exchange(): lax.all_to_all(shaped, axes, split_axis=0, concat_axis=0, tiled=True)]
    pallas_call x6, Pallas kernels: 13.5 us -> 14.8 us  [call(): pl.pallas_call(body, out_shape=[jax.ShapeDtypeStruct(s, d) for s, d in ou...]
  transfers between devices with their start and end apart: 1 -> 1, of which waited for: 1 -> 1; matrix products, arithmetic and copies ran while one was open for 0% -> 0% of each run, Pallas kernels for 4% -> 5%
where the time goes in v3:
time: 79.7 us; the launch traced here: 79.4 us
  blocking collectives  49.4 us (62%)
  Pallas kernels  14.8 us (19%)
  starting transfers between devices  7.33 us (9%)
  waiting for transfers between devices  6.31 us (8%)
    all_to_all x3, blocking collectives, exchange(): lax.all_to_all(shaped, axes, split_axis=0, concat_axis=0, tiled=True)  49.4 us
    pallas_call x6, Pallas kernels, call(): pl.pallas_call(body, out_shape=[jax.ShapeDtypeStruct(s, d) for s, d in ou...  14.8 us
    all_to_all x1, starting transfers between devices, exchange(): lax.all_to_all(shaped, axes, split_axis=0, concat_axis=0, tiled=True)  7.33 us
    all_to_all x1, waiting for transfers between devices, exchange(): lax.all_to_all(shaped, axes, split_axis=0, concat_axis=0, tiled=True)  6.31 us
  transfers between devices with their start and end apart: 1, of which 1 were waited for; matrix products, arithmetic and copies ran while one was open for 0% of the time, Pallas kernels for 5%

profile of v3, /device:TPU:0, one launch (start us, length us, event | category | flops | bytes accessed | tf_op | source)
XLA Modules:
  0.0 79.4 jit_solution(1665575100440435510)
XLA Ops:
  0.6 2.2 %synthesis_kernel.1 = bf16[2,2,128,256]{3,2,1,0:T(8,128)(2,1)} custom-call(bf16[2,64,256]{2,1,0:T(8,128)(2,1)} %refs_4_.5, bf16[2,64,128]{2,1,0:T(8,128)(2,1)} %bitcast.22, bf16[256,256]{1,0:T(8,128)(2,1)} %constant.37.refs_2_, bf16[256,256]{1,0:T(8,128)(2,1)} %constant.30.clone.refs_3_.refs_1_), custom_call_target="tpu_custom_call" | custom-call | bytes 360448 | tf_op jit(solution)/shard_map/synthesis_kernel/pallas_call | solution.py:400
  2.8 7.3 %all-to-all-start = ((bf16[32,16,256]{2,1,0:T(8,128)(2,1)}), bf16[32,16,256]{2,1,0:T(8,128)(2,1)S(1)}, u32[]{:S(2)}, u32[]{:S(2)}) async-start(bf16[32,16,256]{2,1,0:T(8,128)(2,1)} %bitcast.1), calls=%async_computation | async-start | bytes 524288 | tf_op jit(solution)/shard_map/all_to_all | solution.py:124
  10.2 0.1 pad_add_fusion.refs_0_
  10.2 4.1 %routing_kernel.1 = (bf16[2048,512]{1,0:T(8,128)(2,1)S(1)}, bf16[2,512,256]{2,1,0:T(8,128)(2,1)S(1)}, bf16[512,256]{1,0:T(8,128)(2,1)S(1)}) custom-call(s32[3]{0:T(128)S(1)} %pad_add_fusion.refs_0_, s32[64,128]{1,0:T(8,128)} %bitcast.23, s32[64,128]{1,0:T(8,128)} %bitcast.24, s32[64,128]{1,0:T(8,128)} %bitcast.25, bf16[8,256,512]{2,1,0:T(8,128)(2,1)} %refs_4_.3, ...), custom_call_target="tpu_custom_call" | custom-call | flops 2147483648 | bytes 2719756 | tf_op jit(solution)/shard_map/routing_kernel/pallas_call | solution.py:400
  14.3 0.0 copy-start.7
  14.3 0.7 copy-done.7
  15.0 6.3 %all-to-all-done = bf16[32,16,256]{2,1,0:T(8,128)(2,1)S(1)} async-done(((bf16[32,16,256]{2,1,0:T(8,128)(2,1)}), bf16[32,16,256]{2,1,0:T(8,128)(2,1)S(1)}, u32[]{:S(2)}, u32[]{:S(2)}) %all-to-all-start) | async-done | bytes 262176 | tf_op jit(solution)/shard_map/all_to_all | solution.py:124
  21.3 0.0 copy-done.3
  21.3 0.0 copy-done.11
  21.3 2.5 %neutral_kernel.1 = bf16[16,2,16,1024]{3,2,1,0:T(8,128)(2,1)S(1)} custom-call(bf16[512,256]{1,0:T(8,128)(2,1)S(1)} %bitcast.18, bf16[512,512]{1,0:T(8,128)(2,1)S(1)} %copy-done.3, bf16[256,256]{1,0:T(8,128)(2,1)S(1)} %copy-done.11, bf16[2048,512]{1,0:T(8,128)(2,1)S(1)} %get-tuple-element.7.refs_3_, bf16[2,512,256]{2,1,0:T(8,128)(2,1)S(1)} %get-tuple-element.8.refs_4_), custom_call_target="tpu_custom_call" | custom-call | bytes 3538944 | tf_op jit(solution)/shard_map/neutral_kernel/pallas_call | solution.py:400
  23.9 0.0 copy-start
  23.9 0.0 copy-start.1
  23.9 18.2 %all_to_all.20 = bf16[16,32,1024]{2,1,0:T(8,128)(2,1)S(1)} all-to-all(bf16[16,32,1024]{2,1,0:T(8,128)(2,1)S(1)} %bitcast.17), channel_id=1, replica_groups=mesh['grp'=2,'hold'=2,'rest'=8,'lev'=1] {'grp','rest'}, dimensions={0} | all-to-all | bytes 2097152 | tf_op jit(solution)/shard_map/all_to_all | solution.py:124
  42.1 0.0 copy-done.8
  42.2 0.0 copy-start.2
  42.2 0.0 copy-start.10
  42.2 1.8 %tube_kernel.1 = (f32[4,256,256]{2,1,0:T(8,128)}, bf16[512,1024]{1,0:T(8,128)(2,1)S(1)}) custom-call(bf16[512,1024]{1,0:T(8,128)(2,1)S(1)} %bitcast.15, bf16[512,256]{1,0:T(8,128)(2,1)S(1)} %copy-done.8, f32[4,256,256]{2,1,0:T(8,128)S(1)} %copy-done, f32[256,256]{1,0:T(8,128)S(1)} %copy-done.6, f32[4,256,256]{2,1,0:T(8,128)S(1)} %copy-done.1), custom_call_target="tpu_custom_call" | custom-call | bytes 3670016 | tf_op jit(solution)/shard_map/tube_kernel/pallas_call | solution.py:400
  44.0 18.2 %all_to_all.21 = bf16[16,32,1024]{2,1,0:T(8,128)(2,1)S(1)} all-to-all(bf16[16,32,1024]{2,1,0:T(8,128)(2,1)S(1)} %bitcast.21), channel_id=1, replica_groups=mesh['grp'=2,'hold'=2,'rest'=8,'lev'=1] {'grp','rest'}, dimensions={0} | all-to-all | bytes 2097152 | tf_op jit(solution)/shard_map/all_to_all | solution.py:124
  62.2 0.0 copy-start.9
  62.2 0.0 copy-start.12
  62.2 3.1 %tendency_kernel.1 = bf16[512,256]{1,0:T(8,128)(2,1)S(1)} custom-call(bf16[16,2,16,1024]{3,2,1,0:T(8,128)(2,1)S(1)} %bitcast.16, bf16[512,512]{1,0:T(8,128)(2,1)S(1)} %copy-done.2, bf16[128,768]{1,0:T(8,128)(2,1)S(1)} %copy-done.10, bf16[2048,512]{1,0:T(8,128)(2,1)S(1)} %get-tuple-element.7.refs_3_, bf16[2,512,256]{2,1,0:T(8,128)(2,1)S(1)} %get-tuple-element.8.refs_4_), custom_call_target="tpu_custom_call" | custom-call | bytes 4390912 | tf_op jit(solution)/shard_map/tendency_kernel/pallas_call | solution.py:400
  65.3 12.9 %all_to_all.22 = bf16[32,16,256]{2,1,0:T(8,128)(2,1)S(1)} all-to-all(bf16[32,16,256]{2,1,0:T(8,128)(2,1)S(1)} %bitcast.19), channel_id=1, replica_groups=mesh['grp'=2,'hold'=2,'rest'=8,'lev'=1] {'grp','hold','rest'}, dimensions={0} | all-to-all | bytes 524288 | tf_op jit(solution)/shard_map/all_to_all | solution.py:124
  78.2 0.0 copy-done.4
  78.2 1.1 %analysis_kernel.1 = f32[2,64,256]{2,1,0:T(8,128)} custom-call(bf16[2,2,128,256]{3,2,1,0:T(8,128)(2,1)S(1)} %bitcast.20, bf16[256,256]{1,0:T(8,128)(2,1)S(1)} %copy-done.5, bf16[256,256]{1,0:T(8,128)(2,1)S(1)} %copy-done.4, bf16[2,64,128]{2,1,0:T(8,128)(2,1)S(1)} %copy-done.12, bf16[2,64,256]{2,1,0:T(8,128)(2,1)S(1)} %copy-done.9), custom_call_target="tpu_custom_call" | custom-call | bytes 622592 | tf_op jit(solution)/shard_map/analysis_kernel/pallas_call | solution.py:400
  (14 shorter events, 0.0 us)
Async XLA Ops:
  2.8 18.5 %all-to-all-start = ((bf16[32,16,256]{2,1,0:T(8,128)(2,1)}), bf16[32,16,256]{2,1,0:T(8,128)(2,1)S(1)}, u32[]{:S(2)}, u32[]{:S(2)}) async-start(bf16[32,16,256]{2,1,0:T(8,128)(2,1)} %bitcast.1), calls=%async_computation | async-start | bytes 524288 | tf_op jit(solution)/shard_map/all_to_all | solution.py:124
  10.2 11.1 %copy-start.3 = (bf16[512,512]{1,0:T(8,128)(2,1)S(1)}, bf16[512,512]{1,0:T(8,128)(2,1)}, u32[]{:S(2)}) copy-start(bf16[512,512]{1,0:T(8,128)(2,1)} %constant.32.clone.refs_1_) | copy-start | bytes 1572868
  10.2 11.1 %copy-start.11 = (bf16[256,256]{1,0:T(8,128)(2,1)S(1)}, bf16[256,256]{1,0:T(8,128)(2,1)}, u32[]{:S(2)}) copy-start(bf16[256,256]{1,0:T(8,128)(2,1)} %constant.27.clone.refs_2_) | copy-start | bytes 393220
  14.3 0.7 copy-start.7
  21.3 20.8 %copy-start.6 = (f32[256,256]{1,0:T(8,128)S(1)}, f32[256,256]{1,0:T(8,128)}, u32[]{:S(2)}) copy-start(f32[256,256]{1,0:T(8,128)} %refs_3_.3) | copy-start | bytes 786436
  21.3 20.8 %copy-start.8 = (bf16[512,256]{1,0:T(8,128)(2,1)S(1)}, bf16[512,256]{1,0:T(8,128)(2,1)}, u32[]{:S(2)}) copy-start(bf16[512,256]{1,0:T(8,128)(2,1)} %copy-done.7) | copy-start | bytes 786436
  23.9 18.3 %copy-start = (f32[4,256,256]{2,1,0:T(8,128)S(1)}, f32[4,256,256]{2,1,0:T(8,128)}, u32[]{:S(2)}) copy-start(f32[4,256,256]{2,1,0:T(8,128)} %refs_2_.3) | copy-start | bytes 3145732
  23.9 18.2 %copy-start.1 = (f32[4,256,256]{2,1,0:T(8,128)S(1)}, f32[4,256,256]{2,1,0:T(8,128)}, u32[]{:S(2)}) copy-start(f32[4,256,256]{2,1,0:T(8,128)} %refs_4_.4) | copy-start | bytes 3145732
  42.2 20.1 %copy-start.2 = (bf16[512,512]{1,0:T(8,128)(2,1)S(1)}, bf16[512,512]{1,0:T(8,128)(2,1)}, u32[]{:S(2)}) copy-start(bf16[512,512]{1,0:T(8,128)(2,1)} %constant.33.clone.refs_1_) | copy-start | bytes 1572868
  42.2 20.0 %copy-start.10 = (bf16[128,768]{1,0:T(8,128)(2,1)S(1)}, bf16[128,768]{1,0:T(8,128)(2,1)}, u32[]{:S(2)}) copy-start(bf16[128,768]{1,0:T(8,128)(2,1)} %constant.28.clone.refs_2_) | copy-start | bytes 589828
  62.2 16.0 %copy-start.4 = (bf16[256,256]{1,0:T(8,128)(2,1)S(1)}, bf16[256,256]{1,0:T(8,128)(2,1)}, u32[]{:S(2)}) copy-start(bf16[256,256]{1,0:T(8,128)(2,1)} %constant.37.refs_2_) | copy-start | bytes 393220
  62.2 16.0 %copy-start.5 = (bf16[256,256]{1,0:T(8,128)(2,1)S(1)}, bf16[256,256]{1,0:T(8,128)(2,1)}, u32[]{:S(2)}) copy-start(bf16[256,256]{1,0:T(8,128)(2,1)} %constant.30.clone.refs_3_.refs_1_) | copy-start | bytes 393220
  62.2 16.0 %copy-start.9 = (bf16[2,64,256]{2,1,0:T(8,128)(2,1)S(1)}, bf16[2,64,256]{2,1,0:T(8,128)(2,1)}, u32[]{:S(2)}) copy-start(bf16[2,64,256]{2,1,0:T(8,128)(2,1)} %refs_4_.5) | copy-start | bytes 196612
  62.2 16.0 %copy-start.12 = (bf16[2,64,128]{2,1,0:T(8,128)(2,1)S(1)}, bf16[2,64,128]{2,1,0:T(8,128)(2,1)}, u32[]{:S(2)}) copy-start(bf16[2,64,128]{2,1,0:T(8,128)(2,1)} %refs_3_.4) | copy-start | bytes 98308

commit v4 on v3

--- a/solution.py
+++ b/solution.py
@@ -59,7 +59,14 @@
         self.levels = self.columns // (2 * self.fields)
         self.width = self.block // self.levels
         self.lon_blocks = LON // self.width
-        self.lon_pad = -(-self.lon_blocks // 16) * 16
+        fits = [
+            n
+            for n in range(1, self.lat_local + 1)
+            if self.lat_local % n == 0 and n * self.lon_blocks % 8 == 0
+        ]
+        self.pack = fits[0] if fits else 1
+        self.lon_pad = self.lon_blocks if fits else -(-self.lon_blocks // 8) * 8
+        self.unit = self.pack * self.lon_pad
         self.capacity = 2 * self.tubes // self.sources
         self.slots = self.sources * self.capacity
         self.slots_held = self.members * self.capacity
@@ -92,26 +99,22 @@
     return index.transpose(1, 3, 2, 0, 4)
 
 
-def latitude_rows(plan):
-    p = plan
-    index = np.arange(p.rows_sent).reshape(p.sources, p.copies, p.wave_local, p.lat_local)
-    return index.transpose(1, 3, 0, 2)
-
-
-def inverse_rows(plan):
-    p = plan
-    index = np.arange(p.rows_sent).reshape(p.copies, p.lat_local, p.sources, p.wave_local)
-    return index.transpose(2, 0, 3, 1)
+def strided_rows(plan, part, lat, wave):
+    copy, local = lat // plan.lat_local, lat % plan.lat_local
+    start = (copy * plan.wave_local + wave) * plan.lat_local + local + part * plan.rows_sent
+    return pl.ds(start, plan.sources, stride=plan.copies * plan.wave_local * plan.lat_local)
 
 
 def fourier_tables(plan):
-    wave = np.arange(plan.waves)
+    wave = np.arange(plan.waves).reshape(plan.sources, plan.wave_local).T.reshape(-1)
     lon = np.arange(LON)
     angle = 2.0 * math.pi * ((wave[:, None] * lon[None, :]) % LON) / LON
     full = np.stack([np.cos(angle), -np.sin(angle)], 0)
     full = full.reshape(2, plan.waves, plan.lon_blocks, plan.width)
     full = np.pad(full, ((0, 0), (0, 0), (0, plan.lon_pad - plan.lon_blocks), (0, 0)))
-    forward = full.transpose(3, 2, 0, 1).reshape(plan.width * plan.lon_pad, 2 * plan.waves)
+    forward = full.transpose(3, 2, 0, 1)[:, None]
+    forward = np.broadcast_to(forward, (plan.width, plan.pack) + forward.shape[2:])
+    forward = forward.reshape(plan.width * plan.unit, 2 * plan.waves)
     high = forward.astype(BF)
     low = (forward - high.astype(np.float64)).astype(BF)
     synthesis = np.concatenate([high, low], 1)
@@ -187,9 +190,9 @@
         source = ((mine_g * p.copies + copy) * p.rest + mine_l).astype(F32)
         mask = owner == source
         rank = jnp.where(mask, dot(onehot(mask), before), -1.0)
-        chosen = dot(repeat, rank.astype(BF)) == place
-        cell_slot = jnp.where(chosen, cell_all, 0.0)
-        matrix_slot = jnp.where(chosen, matrix_all, 0.0)
+        taken = dot(repeat, rank.astype(BF)) == place
+        cell_slot = jnp.where(taken, cell_all, 0.0)
+        matrix_slot = jnp.where(taken, matrix_all, 0.0)
         row = dot_nt(ones, cell_slot.astype(BF)) + dot_nt(ones, matrix_slot.astype(BF)) * p.cells
         row = row[0:1, :].astype(I32) - 1
         pick_t[copy] = onehot(row == iota((p.table, p.slots_held), 0))
@@ -221,10 +224,15 @@
     return [group == index for index in range(plan.fields)]
 
 
-def chosen_lanes(plan, masks, pieces):
+def pack_masks(plan):
+    member = iota((plan.unit, plan.half), 0) // plan.lon_pad
+    return [member == index for index in range(plan.pack)]
+
+
+def chosen(masks, pieces):
     result = pieces[0]
-    for index in range(1, plan.fields):
-        result = jnp.where(masks[index], pieces[index], result)
+    for mask, piece in zip(masks[1:], pieces[1:]):
+        result = jnp.where(mask, piece, result)
     return result
 
 
@@ -235,33 +243,45 @@
     return pltpu.roll(array, groups * plan.levels, axis=1)
 
 
-def neutral_kernel(plan, wait, arrived, rows, table, weights, pick_t, out, blocks, outcomes):
+def neutral_kernel(plan, wait, arrived, table, weights, pick_t, out, wide, blocks, outcomes):
     p = plan
-    by_lat = dot(rows[...], arrived[...]).astype(BF)
+    for part in range(2):
+        wide[part * p.rows_sent : (part + 1) * p.rows_sent, :] = arrived[
+            :, part * p.half : (part + 1) * p.half
+        ].astype(F32)
     stacks = []
     for lat in range(p.lat_held):
-        part = by_lat[lat * p.waves : (lat + 1) * p.waves, :]
-        stacks.append(jnp.concatenate([part[:, : p.half], part[:, p.half :]], 0))
+        parts = [
+            wide[strided_rows(p, part, lat, wave), :]
+            for part in range(2)
+            for wave in range(p.wave_local)
+        ]
+        stacks.append(jnp.concatenate(parts, 0).astype(BF))
     spectra = jnp.concatenate(stacks, 1)
     spectra = jnp.concatenate([spectra, spectra], 0)
     grid = dot(table[...], spectra) * p.waves ** (-0.5)
     masks = lane_masks(p, p.cells)
+    members = pack_masks(p)
     per = p.fields
     for copy in range(p.copies):
-        lats = range(copy * p.lat_local, (copy + 1) * p.lat_local)
         for step in range(p.width // per):
             pieces = []
             for index in range(per):
-                start = (step * per + index) * p.lon_pad
-                part = grid[start : start + p.lon_pad, :]
-                pieces.append(
-                    jnp.concatenate([part[:, lat * p.half : (lat + 1) * p.half] for lat in lats], 0)
-                )
+                start = (step * per + index) * p.unit
+                packs = []
+                for pack in range(0, p.lat_local, p.pack):
+                    lats = [copy * p.lat_local + pack + member for member in range(p.pack)]
+                    parts = [
+                        grid[start : start + p.unit, lat * p.half : (lat + 1) * p.half]
+                        for lat in lats
+                    ]
+                    packs.append(chosen(members, parts))
+                pieces.append(jnp.concatenate(packs, 0))
             for field in range(p.fields):
                 turned = [rolled(p, pieces[index], index - field) for index in range(per)]
                 first = (copy * p.fields + field) * p.cells
                 blocks[first : first + p.cells, step * p.half : (step + 1) * p.half] = (
-                    chosen_lanes(p, masks, turned).astype(BF)
+                    chosen(masks, turned).astype(BF)
                 )
     values = blocks[...]
     for matrix in range(p.matrices):
@@ -304,7 +324,7 @@
         copy.wait()
 
 
-def tendency_kernel(plan, wait, arrived, rows, table, weights, pick_t, out, sums, spread):
+def tendency_kernel(plan, wait, arrived, table, weights, pick_t, out, sums, spread, wide):
     p = plan
     for copy in range(p.copies):
         taken = arrived[:, copy].reshape(p.slots_held, p.values)
@@ -320,6 +340,7 @@
                 ]
     tendency = dot(sums[...], weights[...])
     masks = lane_masks(p, p.cells)
+    members = pack_masks(p)
     per = p.fields
     for copy in range(p.copies):
         for step in range(p.width // per):
@@ -331,21 +352,28 @@
                 )
             for index in range(per):
                 turned = [rolled(p, pieces[field], field - index) for field in range(p.fields)]
-                mixed = chosen_lanes(p, masks, turned)
-                start = (step * per + index) * p.lon_pad
+                mixed = chosen(masks, turned)
+                start = (step * per + index) * p.unit
                 for lat in range(p.lat_local):
                     held = copy * p.lat_local + lat
-                    spread[
-                        start : start + p.lon_pad, held * p.half : (held + 1) * p.half
-                    ] = mixed[lat * p.lon_pad : (lat + 1) * p.lon_pad, :]
+                    pack, member = lat // p.pack, lat % p.pack
+                    rows = mixed[pack * p.unit : (pack + 1) * p.unit, :]
+                    spread[start : start + p.unit, held * p.half : (held + 1) * p.half] = (
+                        jnp.where(members[member], rows, 0.0) if p.pack > 1 else rows
+                    )
     high, low = split(spread[...])
     analysed = dot(table[...], jnp.concatenate([high, high, low], 0)) * LON ** (-0.5)
-    analysed = analysed.astype(BF)
-    stacks = []
     for lat in range(p.lat_held):
-        lanes = analysed[:, lat * p.half : (lat + 1) * p.half]
-        stacks.append(jnp.concatenate([lanes[: p.waves], lanes[p.waves :]], 1))
-    out[...] = dot(rows[...], jnp.concatenate(stacks, 0)).astype(BF)
+        for part in range(2):
+            for wave in range(p.wave_local):
+                start = (part * p.wave_local + wave) * p.sources
+                wide[strided_rows(p, part, lat, wave), :] = analysed[
+                    start : start + p.sources, lat * p.half : (lat + 1) * p.half
+                ]
+    for part in range(2):
+        out[:, part * p.half : (part + 1) * p.half] = wide[
+            part * p.rows_sent : (part + 1) * p.rows_sent, :
+        ].astype(BF)
 
 
 def analysis_kernel(plan, wait, arrived, rows, order, analysis, spectral, out):
@@ -492,8 +520,9 @@
         p,
         neutral_kernel,
         [(by_slot, BF)],
-        (fourier, chosen_rows(latitude_rows(p), p.rows_sent), forward_table, weights, pick_t),
+        (fourier, forward_table, weights, pick_t),
         scratch=[
+            ((2 * p.rows_sent, p.half), F32),
             ((p.copies * p.fields * p.cells, p.block), BF),
             ((p.copies, p.table, p.values), BF),
         ],
@@ -520,14 +549,14 @@
         [((p.rows_sent, p.columns), BF)],
         (
             contrib.reshape(by_slot),
-            chosen_rows(inverse_rows(p), p.rows_sent),
             backward_table,
             weights,
             pick_t,
         ),
         scratch=[
             ((p.copies * p.fields * p.cells, p.matrices * p.points), BF),
-            ((p.width * p.lon_pad, p.lat_held * p.half), F32),
+            ((p.width * p.unit, p.lat_held * p.half), F32),
+            ((2 * p.rows_sent, p.half), F32),
         ],
     )
     analysed = exchange(sent, ALL, p.sources)

time: 79.7 us -> 78.3 us (0.982)
  Pallas kernels: 14.8 us -> 13.5 us
    pallas_call x6, Pallas kernels: 14.8 us -> 13.5 us  [call(): pl.pallas_call(body, out_shape=[jax.ShapeDtypeStruct(s, d) for s, d in ou...]
where the time goes in v4:
time: 78.3 us; the launch traced here: 78 us
  blocking collectives  49.3 us (63%)
  Pallas kernels  13.5 us (17%)
  starting transfers between devices  7.33 us (9%)
  waiting for transfers between devices  7.06 us (9%)
    all_to_all x3, blocking collectives, exchange(): lax.all_to_all(shaped, axes, split_axis=0, concat_axis=0, tiled=True)  49.3 us
    pallas_call x6, Pallas kernels, call(): pl.pallas_call(body, out_shape=[jax.ShapeDtypeStruct(s, d) for s, d in ou...  13.5 us
    all_to_all x1, starting transfers between devices, exchange(): lax.all_to_all(shaped, axes, split_axis=0, concat_axis=0, tiled=True)  7.33 us
    all_to_all x1, waiting for transfers between devices, exchange(): lax.all_to_all(shaped, axes, split_axis=0, concat_axis=0, tiled=True)  7.06 us
  transfers between devices with their start and end apart: 1, of which 1 were waited for; matrix products, arithmetic and copies ran while one was open for 0% of the time, Pallas kernels for 5%

profile of v4, /device:TPU:0, one launch (start us, length us, event | category | flops | bytes accessed | tf_op | source)
XLA Modules:
  0.0 78.0 jit_solution(9829875413365010944)
XLA Ops:
  0.6 2.2 %synthesis_kernel.1 = bf16[2,2,128,256]{3,2,1,0:T(8,128)(2,1)} custom-call(bf16[2,64,256]{2,1,0:T(8,128)(2,1)} %refs_4_.5, bf16[2,64,128]{2,1,0:T(8,128)(2,1)} %bitcast.22, bf16[256,256]{1,0:T(8,128)(2,1)} %constant.31.refs_2_, bf16[256,256]{1,0:T(8,128)(2,1)} %constant.26.clone.refs_3_.refs_1_), custom_call_target="tpu_custom_call" | custom-call | bytes 360448 | tf_op jit(solution)/shard_map/synthesis_kernel/pallas_call | solution.py:428
  2.8 7.3 %all-to-all-start = ((bf16[32,16,256]{2,1,0:T(8,128)(2,1)}), bf16[32,16,256]{2,1,0:T(8,128)(2,1)S(1)}, u32[]{:S(2)}, u32[]{:S(2)}) async-start(bf16[32,16,256]{2,1,0:T(8,128)(2,1)} %bitcast.1), calls=%async_computation | async-start | bytes 524288 | tf_op jit(solution)/shard_map/all_to_all | solution.py:127
  10.2 0.1 pad_add_fusion.refs_0_
  10.2 0.0 copy-start.7
  10.2 4.0 %routing_kernel.1 = (bf16[2048,512]{1,0:T(8,128)(2,1)S(1)}, bf16[2,384,256]{2,1,0:T(8,128)(2,1)S(1)}, bf16[512,256]{1,0:T(8,128)(2,1)S(1)}) custom-call(s32[3]{0:T(128)S(1)} %pad_add_fusion.refs_0_, s32[64,128]{1,0:T(8,128)} %bitcast.23, s32[64,128]{1,0:T(8,128)} %bitcast.24, s32[64,128]{1,0:T(8,128)} %bitcast.25, bf16[8,256,512]{2,1,0:T(8,128)(2,1)} %refs_4_.3, ...), custom_call_target="tpu_custom_call" | custom-call | flops 2147483648 | bytes 2719756 | tf_op jit(solution)/shard_map/routing_kernel/pallas_call | solution.py:428
  14.3 7.1 %all-to-all-done = bf16[32,16,256]{2,1,0:T(8,128)(2,1)S(1)} async-done(((bf16[32,16,256]{2,1,0:T(8,128)(2,1)}), bf16[32,16,256]{2,1,0:T(8,128)(2,1)S(1)}, u32[]{:S(2)}, u32[]{:S(2)}) %all-to-all-start) | async-done | bytes 262176 | tf_op jit(solution)/shard_map/all_to_all | solution.py:127
  21.3 0.0 copy-done.7
  21.4 2.0 %neutral_kernel.1 = bf16[16,2,16,1024]{3,2,1,0:T(8,128)(2,1)S(1)} custom-call(bf16[512,256]{1,0:T(8,128)(2,1)S(1)} %bitcast.21, bf16[384,256]{1,0:T(8,128)(2,1)S(1)} %copy-done.7, bf16[2048,512]{1,0:T(8,128)(2,1)S(1)} %get-tuple-element.7.refs_2_, bf16[2,384,256]{2,1,0:T(8,128)(2,1)S(1)} %get-tuple-element.8.refs_3_), custom_call_target="tpu_custom_call" | custom-call | bytes 2949120 | tf_op jit(solution)/shard_map/neutral_kernel/pallas_call | solution.py:428
  23.4 18.1 %all_to_all.20 = bf16[16,32,1024]{2,1,0:T(8,128)(2,1)S(1)} all-to-all(bf16[16,32,1024]{2,1,0:T(8,128)(2,1)S(1)} %bitcast.17), channel_id=1, replica_groups=mesh['grp'=2,'hold'=2,'rest'=8,'lev'=1] {'grp','rest'}, dimensions={0} | all-to-all | bytes 2097152 | tf_op jit(solution)/shard_map/all_to_all | solution.py:127
  41.5 0.0 copy-done
  41.5 0.0 copy-done.1
  41.5 0.0 copy-done.5
  41.5 0.0 copy-start.4
  41.5 1.8 %tube_kernel.1 = (f32[4,256,256]{2,1,0:T(8,128)}, bf16[512,1024]{1,0:T(8,128)(2,1)S(1)}) custom-call(bf16[512,1024]{1,0:T(8,128)(2,1)S(1)} %bitcast.15, bf16[512,256]{1,0:T(8,128)(2,1)S(1)} %get-tuple-element.9.refs_1_, f32[4,256,256]{2,1,0:T(8,128)S(1)} %copy-done, f32[256,256]{1,0:T(8,128)S(1)} %copy-done.5, f32[4,256,256]{2,1,0:T(8,128)S(1)} %copy-done.1), custom_call_target="tpu_custom_call" | custom-call | bytes 3670016 | tf_op jit(solution)/shard_map/tube_kernel/pallas_call | solution.py:428
  43.3 18.2 %all_to_all.21 = bf16[16,32,1024]{2,1,0:T(8,128)(2,1)S(1)} all-to-all(bf16[16,32,1024]{2,1,0:T(8,128)(2,1)S(1)} %bitcast.20), channel_id=1, replica_groups=mesh['grp'=2,'hold'=2,'rest'=8,'lev'=1] {'grp','rest'}, dimensions={0} | all-to-all | bytes 2097152 | tf_op jit(solution)/shard_map/all_to_all | solution.py:127
  61.5 0.0 copy-done.4
  61.5 0.0 copy-start.8
  61.5 2.4 %tendency_kernel.1 = bf16[512,256]{1,0:T(8,128)(2,1)S(1)} custom-call(bf16[16,2,16,1024]{3,2,1,0:T(8,128)(2,1)S(1)} %bitcast.16, bf16[128,1152]{1,0:T(8,128)(2,1)S(1)} %copy-done.4, bf16[2048,512]{1,0:T(8,128)(2,1)S(1)} %get-tuple-element.7.refs_2_, bf16[2,384,256]{2,1,0:T(8,128)(2,1)S(1)} %get-tuple-element.8.refs_3_), custom_call_target="tpu_custom_call" | custom-call | bytes 3833856 | tf_op jit(solution)/shard_map/tendency_kernel/pallas_call | solution.py:428
  64.0 12.9 %all_to_all.22 = bf16[32,16,256]{2,1,0:T(8,128)(2,1)S(1)} all-to-all(bf16[32,16,256]{2,1,0:T(8,128)(2,1)S(1)} %bitcast.18), channel_id=1, replica_groups=mesh['grp'=2,'hold'=2,'rest'=8,'lev'=1] {'grp','hold','rest'}, dimensions={0} | all-to-all | bytes 524288 | tf_op jit(solution)/shard_map/all_to_all | solution.py:127
  76.9 0.0 copy-done.2
  76.9 0.0 copy-done.3
  76.9 0.0 copy-done.6
  76.9 0.0 copy-done.8
  76.9 1.1 %analysis_kernel.1 = f32[2,64,256]{2,1,0:T(8,128)} custom-call(bf16[2,2,128,256]{3,2,1,0:T(8,128)(2,1)S(1)} %bitcast.19, bf16[256,256]{1,0:T(8,128)(2,1)S(1)} %copy-done.3, bf16[256,256]{1,0:T(8,128)(2,1)S(1)} %copy-done.2, bf16[2,64,128]{2,1,0:T(8,128)(2,1)S(1)} %copy-done.8, bf16[2,64,256]{2,1,0:T(8,128)(2,1)S(1)} %copy-done.6), custom_call_target="tpu_custom_call" | custom-call | bytes 622592 | tf_op jit(solution)/shard_map/analysis_kernel/pallas_call | solution.py:428
  (6 shorter events, 0.0 us)
Async XLA Ops:
  2.8 18.5 %all-to-all-start = ((bf16[32,16,256]{2,1,0:T(8,128)(2,1)}), bf16[32,16,256]{2,1,0:T(8,128)(2,1)S(1)}, u32[]{:S(2)}, u32[]{:S(2)}) async-start(bf16[32,16,256]{2,1,0:T(8,128)(2,1)} %bitcast.1), calls=%async_computation | async-start | bytes 524288 | tf_op jit(solution)/shard_map/all_to_all | solution.py:127
  10.2 11.1 %copy-start.7 = (bf16[384,256]{1,0:T(8,128)(2,1)S(1)}, bf16[384,256]{1,0:T(8,128)(2,1)}, u32[]{:S(2)}) copy-start(bf16[384,256]{1,0:T(8,128)(2,1)} %constant.23.clone.refs_1_) | copy-start | bytes 589828
  21.3 20.1 %copy-start = (f32[4,256,256]{2,1,0:T(8,128)S(1)}, f32[4,256,256]{2,1,0:T(8,128)}, u32[]{:S(2)}) copy-start(f32[4,256,256]{2,1,0:T(8,128)} %refs_2_.1) | copy-start | bytes 3145732
  21.3 20.1 %copy-start.1 = (f32[4,256,256]{2,1,0:T(8,128)S(1)}, f32[4,256,256]{2,1,0:T(8,128)}, u32[]{:S(2)}) copy-start(f32[4,256,256]{2,1,0:T(8,128)} %refs_4_.4) | copy-start | bytes 3145732
  21.3 20.1 %copy-start.5 = (f32[256,256]{1,0:T(8,128)S(1)}, f32[256,256]{1,0:T(8,128)}, u32[]{:S(2)}) copy-start(f32[256,256]{1,0:T(8,128)} %refs_3_.3) | copy-start | bytes 786436
  41.5 20.0 %copy-start.4 = (bf16[128,1152]{1,0:T(8,128)(2,1)S(1)}, bf16[128,1152]{1,0:T(8,128)(2,1)}, u32[]{:S(2)}) copy-start(bf16[128,1152]{1,0:T(8,128)(2,1)} %constant.24.clone.refs_1_) | copy-start | bytes 884740
  61.5 15.4 %copy-start.2 = (bf16[256,256]{1,0:T(8,128)(2,1)S(1)}, bf16[256,256]{1,0:T(8,128)(2,1)}, u32[]{:S(2)}) copy-start(bf16[256,256]{1,0:T(8,128)(2,1)} %constant.31.refs_2_) | copy-start | bytes 393220
  61.5 15.4 %copy-start.3 = (bf16[256,256]{1,0:T(8,128)(2,1)S(1)}, bf16[256,256]{1,0:T(8,128)(2,1)}, u32[]{:S(2)}) copy-start(bf16[256,256]{1,0:T(8,128)(2,1)} %constant.26.clone.refs_3_.refs_1_) | copy-start | bytes 393220
  61.5 15.4 %copy-start.6 = (bf16[2,64,256]{2,1,0:T(8,128)(2,1)S(1)}, bf16[2,64,256]{2,1,0:T(8,128)(2,1)}, u32[]{:S(2)}) copy-start(bf16[2,64,256]{2,1,0:T(8,128)(2,1)} %refs_4_.5) | copy-start | bytes 196612
  61.5 15.4 %copy-start.8 = (bf16[2,64,128]{2,1,0:T(8,128)(2,1)S(1)}, bf16[2,64,128]{2,1,0:T(8,128)(2,1)}, u32[]{:S(2)}) copy-start(bf16[2,64,128]{2,1,0:T(8,128)(2,1)} %refs_3_.4) | copy-start | bytes 98308

commit v5 on v4

--- a/solution.py
+++ b/solution.py
@@ -128,13 +128,28 @@
     return moved.reshape(array.shape)
 
 
-def synthesis_kernel(plan, wait, spectral, synthesis_t, order, rows, out):
+def synthesis_kernel(plan, wait, spectral, synthesis_t, out):
     p = plan
+    column = iota((1, p.columns), 1)
+    part, rest = column // p.half, column % p.half
+    origin = ((rest % p.levels) * p.fields + rest // p.levels) * 2 + part
+    order = onehot(iota((p.columns, p.columns), 0) == origin)
+    row = iota((p.rows, 1), 0)
+    local, row = row % p.lat_local, row // p.lat_local
+    owner, row = row % p.wave_local, row // p.wave_local
+    copy, row = row % p.copies, row // p.copies
+    rest, group = row % p.rest, row // p.rest
+    latitude = ((group * p.copies + copy) * p.rest + rest) * p.lat_local + local
+    places = []
+    for wave in range(p.wave_local):
+        place = jnp.where(owner == wave, latitude, -1)
+        places.append(onehot(iota((p.rows, p.latitudes), 1) == place))
+    wait(0)
+    wait(1)
     total = 0.0
     for wave in range(p.wave_local):
-        moved = dot(spectral[wave], order[...]).astype(BF)
-        here = rows[:, wave * p.latitudes : (wave + 1) * p.latitudes]
-        placed = dot_nt(here, synthesis_t[wave]).astype(BF)
+        moved = dot(spectral[wave], order).astype(BF)
+        placed = dot_nt(places[wave], synthesis_t[wave]).astype(BF)
         total = total + dot(placed, moved)
     moved = total.astype(BF).reshape(p.grp, p.rows // p.grp, p.columns)
     for copy in range(p.copies):
@@ -338,18 +353,20 @@
                     matrix * p.cells : (matrix + 1) * p.cells,
                     field * p.points : (field + 1) * p.points,
                 ]
-    tendency = dot(sums[...], weights[...])
     masks = lane_masks(p, p.cells)
     members = pack_masks(p)
     per = p.fields
-    for copy in range(p.copies):
-        for step in range(p.width // per):
+    steps = p.width // per
+    group = math.gcd(steps, 2)
+    for step in range(steps):
+        if step % group == 0:
+            tendency = dot(sums[...], weights[:, step * p.half : (step + group) * p.half])
+        lanes = slice(step % group * p.half, (step % group + 1) * p.half)
+        for copy in range(p.copies):
             pieces = []
             for field in range(p.fields):
                 first = (copy * p.fields + field) * p.cells
-                pieces.append(
-                    tendency[first : first + p.cells, step * p.half : (step + 1) * p.half]
-                )
+                pieces.append(tendency[first : first + p.cells, lanes])
             for index in range(per):
                 turned = [rolled(p, pieces[field], field - index) for field in range(p.fields)]
                 mixed = chosen(masks, turned)
@@ -376,16 +393,24 @@
         ].astype(BF)
 
 
-def analysis_kernel(plan, wait, arrived, rows, order, analysis, spectral, out):
+def analysis_kernel(plan, wait, arrived, rows, order, analysis, spectral, out, held, done):
+    p = plan
+    placed = []
+    for wave in range(p.wave_local):
+        here = rows[:, wave * p.latitudes : (wave + 1) * p.latitudes]
+        placed.append(dot_nt(analysis[wave], here).astype(BF))
     joined = arrived[:, 0].astype(F32)
-    for copy in range(1, plan.copies):
+    for copy in range(1, p.copies):
         joined = joined + arrived[:, copy].astype(F32)
-    joined = joined.reshape(plan.rows, plan.columns).astype(BF)
-    natural = dot_tn(rows[...], joined).astype(BF)
-    natural = dot_nt(natural, order[...]).astype(BF)
-    for wave in range(plan.wave_local):
-        part = natural[wave * plan.latitudes : (wave + 1) * plan.latitudes, :]
-        out[wave] = spectral[wave].astype(F32) + dot(analysis[wave], part)
+    joined = joined.reshape(p.rows, p.columns).astype(BF)
+    natural = dot_nt(joined, order[...]).astype(BF)
+    copies = []
+    for wave in range(p.wave_local):
+        held[wave] = spectral[wave].astype(F32) + dot(placed[wave], natural)
+        copies.append(pltpu.make_async_copy(held.at[wave], out.at[wave], done.at[wave]))
+        copies[-1].start()
+    for copy in copies:
+        copy.wait()
 
 
 def call(
@@ -488,8 +513,9 @@
         p,
         synthesis_kernel,
         [((p.grp, p.copies, p.rows // p.grp, p.columns), BF)],
-        (spectral, synthesis.transpose(0, 2, 1), order, wave_order),
-        fetched=(0, 1, 2, 3),
+        (spectral, synthesis.transpose(0, 2, 1)),
+        fetched=(0, 1),
+        late=(0, 1),
     )
     flat = (p.rows_sent, p.columns)
     fourier = exchange(sent.reshape(flat), ALL, p.sources)
@@ -571,6 +597,7 @@
             analysis,
             spectral,
         ),
+        stored=(0,),
     )
     return spectral_new, state
 

time: 78.3 us -> 78.1 us (level)
  no operation moved by 1% of the time
where the time goes in v5:
time: 78.1 us; the launch traced here: 77.8 us
  blocking collectives  49.3 us (63%)
  Pallas kernels  13.3 us (17%)
  starting transfers between devices  7.33 us (9%)
  waiting for transfers between devices  7.05 us (9%)
    all_to_all x3, blocking collectives, exchange(): lax.all_to_all(shaped, axes, split_axis=0, concat_axis=0, tiled=True)  49.3 us
    pallas_call x6, Pallas kernels, call(): pl.pallas_call(body, out_shape=[jax.ShapeDtypeStruct(s, d) for s, d in ou...  13.3 us
    all_to_all x1, starting transfers between devices, exchange(): lax.all_to_all(shaped, axes, split_axis=0, concat_axis=0, tiled=True)  7.33 us
    all_to_all x1, waiting for transfers between devices, exchange(): lax.all_to_all(shaped, axes, split_axis=0, concat_axis=0, tiled=True)  7.05 us
  transfers between devices with their start and end apart: 1, of which 1 were waited for; matrix products, arithmetic and copies ran while one was open for 0% of the time, Pallas kernels for 5%

profile of v5, /device:TPU:0, one launch (start us, length us, event | category | flops | bytes accessed | tf_op | source)
XLA Modules:
  0.0 77.8 jit_solution(4226451335029178134)
XLA Ops:
  0.6 2.0 %synthesis_kernel.1 = bf16[2,2,128,256]{3,2,1,0:T(8,128)(2,1)} custom-call(bf16[2,64,256]{2,1,0:T(8,128)(2,1)} %refs_4_.5, bf16[2,64,128]{2,1,0:T(8,128)(2,1)} %bitcast.22), custom_call_target="tpu_custom_call" | custom-call | bytes 98304 | tf_op jit(solution)/shard_map/synthesis_kernel/pallas_call | solution.py:453
  2.6 7.3 %all-to-all-start = ((bf16[32,16,256]{2,1,0:T(8,128)(2,1)}), bf16[32,16,256]{2,1,0:T(8,128)(2,1)S(1)}, u32[]{:S(2)}, u32[]{:S(2)}) async-start(bf16[32,16,256]{2,1,0:T(8,128)(2,1)} %bitcast.1), calls=%async_computation | async-start | bytes 524288 | tf_op jit(solution)/shard_map/all_to_all | solution.py:127
  9.9 0.1 pad_add_fusion.refs_0_
  10.0 0.0 copy-start.5
  10.0 4.0 %routing_kernel.1 = (bf16[2048,512]{1,0:T(8,128)(2,1)S(1)}, bf16[2,384,256]{2,1,0:T(8,128)(2,1)S(1)}, bf16[512,256]{1,0:T(8,128)(2,1)S(1)}) custom-call(s32[3]{0:T(128)S(1)} %pad_add_fusion.refs_0_, s32[64,128]{1,0:T(8,128)} %bitcast.23, s32[64,128]{1,0:T(8,128)} %bitcast.24, s32[64,128]{1,0:T(8,128)} %bitcast.25, bf16[8,256,512]{2,1,0:T(8,128)(2,1)} %refs_4_.3, ...), custom_call_target="tpu_custom_call" | custom-call | flops 2147483648 | bytes 2719756 | tf_op jit(solution)/shard_map/routing_kernel/pallas_call | solution.py:453
  14.1 7.1 %all-to-all-done = bf16[32,16,256]{2,1,0:T(8,128)(2,1)S(1)} async-done(((bf16[32,16,256]{2,1,0:T(8,128)(2,1)}), bf16[32,16,256]{2,1,0:T(8,128)(2,1)S(1)}, u32[]{:S(2)}, u32[]{:S(2)}) %all-to-all-start) | async-done | bytes 262176 | tf_op jit(solution)/shard_map/all_to_all | solution.py:127
  21.1 0.0 copy-done.5
  21.1 2.0 %neutral_kernel.1 = bf16[16,2,16,1024]{3,2,1,0:T(8,128)(2,1)S(1)} custom-call(bf16[512,256]{1,0:T(8,128)(2,1)S(1)} %bitcast.21, bf16[384,256]{1,0:T(8,128)(2,1)S(1)} %copy-done.5, bf16[2048,512]{1,0:T(8,128)(2,1)S(1)} %get-tuple-element.7.refs_2_, bf16[2,384,256]{2,1,0:T(8,128)(2,1)S(1)} %get-tuple-element.8.refs_3_), custom_call_target="tpu_custom_call" | custom-call | bytes 2949120 | tf_op jit(solution)/shard_map/neutral_kernel/pallas_call | solution.py:453
  23.2 18.1 %all_to_all.20 = bf16[16,32,1024]{2,1,0:T(8,128)(2,1)S(1)} all-to-all(bf16[16,32,1024]{2,1,0:T(8,128)(2,1)S(1)} %bitcast.17), channel_id=1, replica_groups=mesh['grp'=2,'hold'=2,'rest'=8,'lev'=1] {'grp','rest'}, dimensions={0} | all-to-all | bytes 2097152 | tf_op jit(solution)/shard_map/all_to_all | solution.py:127
  41.2 0.0 copy-done
  41.2 0.0 copy-done.1
  41.2 0.0 copy-done.3
  41.3 0.0 copy-start.2
  41.3 1.8 %tube_kernel.1 = (f32[4,256,256]{2,1,0:T(8,128)}, bf16[512,1024]{1,0:T(8,128)(2,1)S(1)}) custom-call(bf16[512,1024]{1,0:T(8,128)(2,1)S(1)} %bitcast.15, bf16[512,256]{1,0:T(8,128)(2,1)S(1)} %get-tuple-element.9.refs_1_, f32[4,256,256]{2,1,0:T(8,128)S(1)} %copy-done, f32[256,256]{1,0:T(8,128)S(1)} %copy-done.3, f32[4,256,256]{2,1,0:T(8,128)S(1)} %copy-done.1), custom_call_target="tpu_custom_call" | custom-call | bytes 3670016 | tf_op jit(solution)/shard_map/tube_kernel/pallas_call | solution.py:453
  43.0 18.2 %all_to_all.21 = bf16[16,32,1024]{2,1,0:T(8,128)(2,1)S(1)} all-to-all(bf16[16,32,1024]{2,1,0:T(8,128)(2,1)S(1)} %bitcast.20), channel_id=1, replica_groups=mesh['grp'=2,'hold'=2,'rest'=8,'lev'=1] {'grp','rest'}, dimensions={0} | all-to-all | bytes 2097152 | tf_op jit(solution)/shard_map/all_to_all | solution.py:127
  61.3 0.0 copy-done.2
  61.3 0.0 copy-start.8
  61.3 2.4 %tendency_kernel.1 = bf16[512,256]{1,0:T(8,128)(2,1)S(1)} custom-call(bf16[16,2,16,1024]{3,2,1,0:T(8,128)(2,1)S(1)} %bitcast.16, bf16[128,1152]{1,0:T(8,128)(2,1)S(1)} %copy-done.2, bf16[2048,512]{1,0:T(8,128)(2,1)S(1)} %get-tuple-element.7.refs_2_, bf16[2,384,256]{2,1,0:T(8,128)(2,1)S(1)} %get-tuple-element.8.refs_3_), custom_call_target="tpu_custom_call" | custom-call | bytes 3833856 | tf_op jit(solution)/shard_map/tendency_kernel/pallas_call | solution.py:453
  63.7 12.9 %all_to_all.22 = bf16[32,16,256]{2,1,0:T(8,128)(2,1)S(1)} all-to-all(bf16[32,16,256]{2,1,0:T(8,128)(2,1)S(1)} %bitcast.18), channel_id=1, replica_groups=mesh['grp'=2,'hold'=2,'rest'=8,'lev'=1] {'grp','hold','rest'}, dimensions={0} | all-to-all | bytes 524288 | tf_op jit(solution)/shard_map/all_to_all | solution.py:127
  76.7 0.0 copy-done.4
  76.7 0.0 copy-done.6
  76.7 0.0 copy-done.7
  76.7 0.0 copy-done.8
  76.7 1.1 %analysis_kernel.1 = f32[2,64,256]{2,1,0:T(8,128)} custom-call(bf16[2,2,128,256]{3,2,1,0:T(8,128)(2,1)S(1)} %bitcast.19, bf16[256,256]{1,0:T(8,128)(2,1)S(1)} %copy-done.7, bf16[256,256]{1,0:T(8,128)(2,1)S(1)} %copy-done.6, bf16[2,64,128]{2,1,0:T(8,128)(2,1)S(1)} %copy-done.8, bf16[2,64,256]{2,1,0:T(8,128)(2,1)S(1)} %copy-done.4), custom_call_target="tpu_custom_call" | custom-call | bytes 622592 | tf_op jit(solution)/shard_map/analysis_kernel/pallas_call | solution.py:453
  (6 shorter events, 0.0 us)
Async XLA Ops:
  2.6 18.5 %all-to-all-start = ((bf16[32,16,256]{2,1,0:T(8,128)(2,1)}), bf16[32,16,256]{2,1,0:T(8,128)(2,1)S(1)}, u32[]{:S(2)}, u32[]{:S(2)}) async-start(bf16[32,16,256]{2,1,0:T(8,128)(2,1)} %bitcast.1), calls=%async_computation | async-start | bytes 524288 | tf_op jit(solution)/shard_map/all_to_all | solution.py:127
  10.0 11.1 %copy-start.5 = (bf16[384,256]{1,0:T(8,128)(2,1)S(1)}, bf16[384,256]{1,0:T(8,128)(2,1)}, u32[]{:S(2)}) copy-start(bf16[384,256]{1,0:T(8,128)(2,1)} %constant.23.clone.refs_1_) | copy-start | bytes 589828
  21.1 20.1 %copy-start = (f32[4,256,256]{2,1,0:T(8,128)S(1)}, f32[4,256,256]{2,1,0:T(8,128)}, u32[]{:S(2)}) copy-start(f32[4,256,256]{2,1,0:T(8,128)} %refs_2_.1) | copy-start | bytes 3145732
  21.1 20.1 %copy-start.1 = (f32[4,256,256]{2,1,0:T(8,128)S(1)}, f32[4,256,256]{2,1,0:T(8,128)}, u32[]{:S(2)}) copy-start(f32[4,256,256]{2,1,0:T(8,128)} %refs_4_.4) | copy-start | bytes 3145732
  21.1 20.1 %copy-start.3 = (f32[256,256]{1,0:T(8,128)S(1)}, f32[256,256]{1,0:T(8,128)}, u32[]{:S(2)}) copy-start(f32[256,256]{1,0:T(8,128)} %refs_3_.2) | copy-start | bytes 786436
  41.3 20.0 %copy-start.2 = (bf16[128,1152]{1,0:T(8,128)(2,1)S(1)}, bf16[128,1152]{1,0:T(8,128)(2,1)}, u32[]{:S(2)}) copy-start(bf16[128,1152]{1,0:T(8,128)(2,1)} %constant.24.clone.refs_1_) | copy-start | bytes 884740
  61.3 15.4 %copy-start.4 = (bf16[2,64,256]{2,1,0:T(8,128)(2,1)S(1)}, bf16[2,64,256]{2,1,0:T(8,128)(2,1)}, u32[]{:S(2)}) copy-start(bf16[2,64,256]{2,1,0:T(8,128)(2,1)} %refs_4_.5) | copy-start | bytes 196612
  61.3 15.4 %copy-start.6 = (bf16[256,256]{1,0:T(8,128)(2,1)S(1)}, bf16[256,256]{1,0:T(8,128)(2,1)}, u32[]{:S(2)}) copy-start(bf16[256,256]{1,0:T(8,128)(2,1)} %constant.32.refs_2_) | copy-start | bytes 393220
  61.3 15.4 %copy-start.7 = (bf16[256,256]{1,0:T(8,128)(2,1)S(1)}, bf16[256,256]{1,0:T(8,128)(2,1)}, u32[]{:S(2)}) copy-start(bf16[256,256]{1,0:T(8,128)(2,1)} %constant.26.clone.refs_1_) | copy-start | bytes 393220
  61.3 15.4 %copy-start.8 = (bf16[2,64,128]{2,1,0:T(8,128)(2,1)S(1)}, bf16[2,64,128]{2,1,0:T(8,128)(2,1)}, u32[]{:S(2)}) copy-start(bf16[2,64,128]{2,1,0:T(8,128)(2,1)} %refs_3_.3) | copy-start | bytes 98308

commit v6 on v5

--- a/solution.py
+++ b/solution.py
@@ -316,10 +316,9 @@
 
 
 def tube_kernel(
-    plan, wait, arrived, seat_t, tube_state, collision, inverse, state_out, out, drag, held, done
+    plan, wait, arrived, seat_t, tube_state, collision, inverse, state_out, out, drag
 ):
     neutral = dot_tn(seat_t[...], arrived[...])
-    copies = []
     for field in range(plan.fields):
         lanes = slice(field * plan.points, (field + 1) * plan.points)
         wind = neutral[:, lanes]
@@ -328,19 +327,17 @@
         state = dot_nt(force_high, inverse_high) + (
             dot_nt(force_high, inverse_low) + dot_nt(force_low, inverse_high)
         )
-        held[field] = state
-        copies.append(
-            pltpu.make_async_copy(held.at[field], state_out.at[field], done.at[field])
-        )
-        copies[-1].start()
+        state_out[field] = state
         drag[:, lanes] = (collision[...] * (state - wind)).astype(BF)
     out[...] = dot(seat_t[...], drag[...]).astype(BF)
-    for copy in copies:
-        copy.wait()
-
-
-def tendency_kernel(plan, wait, arrived, table, weights, pick_t, out, sums, spread, wide):
+
+
+def tendency_kernel(
+    plan, wait, arrived, table, weights, pick_t, state, out, state_out, sums, spread, wide, done
+):
     p = plan
+    store = pltpu.make_async_copy(state, state_out, done)
+    store.start()
     for copy in range(p.copies):
         taken = arrived[:, copy].reshape(p.slots_held, p.values)
         found = dot(pick_t[copy], taken).astype(BF)
@@ -391,6 +388,7 @@
         out[:, part * p.half : (part + 1) * p.half] = wide[
             part * p.rows_sent : (part + 1) * p.rows_sent, :
         ].astype(BF)
+    store.wait()
 
 
 def analysis_kernel(plan, wait, arrived, rows, order, analysis, spectral, out, held, done):
@@ -414,7 +412,7 @@
 
 
 def call(
-    plan, kernel, outs, operands, scratch=(), smem=0, fetched=(), late=(), stored=(), flops=0
+    plan, kernel, outs, operands, scratch=(), smem=0, fetched=(), late=(), stored=(), handed=(), flops=0
 ):
     vmem = pl.BlockSpec(memory_space=pltpu.VMEM)
     hbm = pl.BlockSpec(memory_space=pltpu.HBM)
@@ -430,6 +428,8 @@
     held = [pltpu.VMEM(s, d) for s, d in scratch]
     for i in stored:
         held += [pltpu.VMEM(*outs[i]), pltpu.SemaphoreType.DMA(outs[i][0][:1])]
+    if handed:
+        held += [pltpu.SemaphoreType.DMA(())]
     if fetched:
         held += [pltpu.VMEM(operands[i].shape, operands[i].dtype) for i in fetched]
         held += [pltpu.SemaphoreType.DMA((len(fetched),))]
@@ -454,7 +454,7 @@
         body,
         out_shape=[jax.ShapeDtypeStruct(s, d) for s, d in outs],
         in_specs=in_specs,
-        out_specs=[hbm if i in stored else vmem for i in range(len(outs))],
+        out_specs=[hbm if i in stored + handed else vmem for i in range(len(outs))],
         scratch_shapes=held,
         cost_estimate=pl.CostEstimate(flops=flops, bytes_accessed=size, transcendentals=0),
         compiler_params=pltpu.CompilerParams(vmem_limit_bytes=VMEM_LIMIT),
@@ -561,7 +561,6 @@
             [(tube_state.shape, F32), (flat, BF)],
             (arrived, seat_t, tube_state, collision, block_inverse),
             scratch=[((p.tubes, p.values), BF)],
-            stored=(0,),
         )
     else:
         state, wind = swept(p, dot_tn(seat_t, arrived), tube_state, end_coupling, block_inverse)
@@ -569,21 +568,23 @@
         drag = drag.transpose(1, 0, 2).reshape(p.tubes, p.values)
         sent = dot(seat_t, drag).astype(BF)
     contrib = exchange(sent, GROUP, p.members)
-    (sent,) = call(
+    sent, state = call(
         p,
         tendency_kernel,
-        [((p.rows_sent, p.columns), BF)],
+        [((p.rows_sent, p.columns), BF), (state.shape, F32)],
         (
             contrib.reshape(by_slot),
             backward_table,
             weights,
             pick_t,
+            state,
         ),
         scratch=[
             ((p.copies * p.fields * p.cells, p.matrices * p.points), BF),
             ((p.width * p.unit, p.lat_held * p.half), F32),
             ((2 * p.rows_sent, p.half), F32),
         ],
+        handed=(1,),
     )
     analysed = exchange(sent, ALL, p.sources)
     (spectral_new,) = call(

time: 78.1 us -> 77.5 us (level)
  no operation moved by 1% of the time
where the time goes in v6:
time: 77.5 us; the launch traced here: 77.2 us
  blocking collectives  49.3 us (64%)
  Pallas kernels  12.7 us (16%)
  starting transfers between devices  7.33 us (9%)
  waiting for transfers between devices  7.05 us (9%)
    all_to_all x3, blocking collectives, exchange(): lax.all_to_all(shaped, axes, split_axis=0, concat_axis=0, tiled=True)  49.3 us
    pallas_call x6, Pallas kernels, call(): pl.pallas_call(body, out_shape=[jax.ShapeDtypeStruct(s, d) for s, d in ou...  12.7 us
    all_to_all x1, starting transfers between devices, exchange(): lax.all_to_all(shaped, axes, split_axis=0, concat_axis=0, tiled=True)  7.33 us
    all_to_all x1, waiting for transfers between devices, exchange(): lax.all_to_all(shaped, axes, split_axis=0, concat_axis=0, tiled=True)  7.05 us
  transfers between devices with their start and end apart: 1, of which 1 were waited for; matrix products, arithmetic and copies ran while one was open for 0% of the time, Pallas kernels for 5%

profile of v6, /device:TPU:0, one launch (start us, length us, event | category | flops | bytes accessed | tf_op | source)
XLA Modules:
  0.0 77.2 jit_solution(317604274961774018)
XLA Ops:
  0.6 2.0 %synthesis_kernel.1 = bf16[2,2,128,256]{3,2,1,0:T(8,128)(2,1)} custom-call(bf16[2,64,256]{2,1,0:T(8,128)(2,1)} %refs_4_.5, bf16[2,64,128]{2,1,0:T(8,128)(2,1)} %bitcast.22), custom_call_target="tpu_custom_call" | custom-call | bytes 98304 | tf_op jit(solution)/shard_map/synthesis_kernel/pallas_call | solution.py:453
  2.6 7.3 %all-to-all-start = ((bf16[32,16,256]{2,1,0:T(8,128)(2,1)}), bf16[32,16,256]{2,1,0:T(8,128)(2,1)S(1)}, u32[]{:S(2)}, u32[]{:S(2)}) async-start(bf16[32,16,256]{2,1,0:T(8,128)(2,1)} %bitcast.1), calls=%async_computation | async-start | bytes 524288 | tf_op jit(solution)/shard_map/all_to_all | solution.py:127
  9.9 0.1 pad_add_fusion.refs_0_
  10.0 0.0 copy-start.5
  10.0 4.0 %routing_kernel.1 = (bf16[2048,512]{1,0:T(8,128)(2,1)S(1)}, bf16[2,384,256]{2,1,0:T(8,128)(2,1)S(1)}, bf16[512,256]{1,0:T(8,128)(2,1)S(1)}) custom-call(s32[3]{0:T(128)S(1)} %pad_add_fusion.refs_0_, s32[64,128]{1,0:T(8,128)} %bitcast.23, s32[64,128]{1,0:T(8,128)} %bitcast.24, s32[64,128]{1,0:T(8,128)} %bitcast.25, bf16[8,256,512]{2,1,0:T(8,128)(2,1)} %refs_4_.3, ...), custom_call_target="tpu_custom_call" | custom-call | flops 2147483648 | bytes 2719756 | tf_op jit(solution)/shard_map/routing_kernel/pallas_call | solution.py:453
  14.1 7.1 %all-to-all-done = bf16[32,16,256]{2,1,0:T(8,128)(2,1)S(1)} async-done(((bf16[32,16,256]{2,1,0:T(8,128)(2,1)}), bf16[32,16,256]{2,1,0:T(8,128)(2,1)S(1)}, u32[]{:S(2)}, u32[]{:S(2)}) %all-to-all-start) | async-done | bytes 262176 | tf_op jit(solution)/shard_map/all_to_all | solution.py:127
  21.1 0.0 copy-done.5
  21.1 2.0 %neutral_kernel.1 = bf16[16,2,16,1024]{3,2,1,0:T(8,128)(2,1)S(1)} custom-call(bf16[512,256]{1,0:T(8,128)(2,1)S(1)} %bitcast.20, bf16[384,256]{1,0:T(8,128)(2,1)S(1)} %copy-done.5, bf16[2048,512]{1,0:T(8,128)(2,1)S(1)} %get-tuple-element.9.refs_2_, bf16[2,384,256]{2,1,0:T(8,128)(2,1)S(1)} %get-tuple-element.10.refs_3_), custom_call_target="tpu_custom_call" | custom-call | bytes 2949120 | tf_op jit(solution)/shard_map/neutral_kernel/pallas_call | solution.py:453
  23.2 18.1 %all_to_all.20 = bf16[16,32,1024]{2,1,0:T(8,128)(2,1)S(1)} all-to-all(bf16[16,32,1024]{2,1,0:T(8,128)(2,1)S(1)} %bitcast.17), channel_id=1, replica_groups=mesh['grp'=2,'hold'=2,'rest'=8,'lev'=1] {'grp','rest'}, dimensions={0} | all-to-all | bytes 2097152 | tf_op jit(solution)/shard_map/all_to_all | solution.py:127
  41.2 0.0 copy-done
  41.2 0.0 copy-done.1
  41.2 0.0 copy-done.3
  41.3 0.0 copy-start.2
  41.3 1.2 %tube_kernel.1 = (f32[4,256,256]{2,1,0:T(8,128)S(1)}, bf16[512,1024]{1,0:T(8,128)(2,1)S(1)}) custom-call(bf16[512,1024]{1,0:T(8,128)(2,1)S(1)} %bitcast.16, bf16[512,256]{1,0:T(8,128)(2,1)S(1)} %get-tuple-element.11.refs_1_, f32[4,256,256]{2,1,0:T(8,128)S(1)} %copy-done, f32[256,256]{1,0:T(8,128)S(1)} %copy-done.3, f32[4,256,256]{2,1,0:T(8,128)S(1)} %copy-done.1), custom_call_target="tpu_custom_call" | custom-call | bytes 3670016 | tf_op jit(solution)/shard_map/tube_kernel/pallas_call | solution.py:453
  42.5 18.2 %all_to_all.21 = bf16[16,32,1024]{2,1,0:T(8,128)(2,1)S(1)} all-to-all(bf16[16,32,1024]{2,1,0:T(8,128)(2,1)S(1)} %bitcast.19), channel_id=1, replica_groups=mesh['grp'=2,'hold'=2,'rest'=8,'lev'=1] {'grp','rest'}, dimensions={0} | all-to-all | bytes 2097152 | tf_op jit(solution)/shard_map/all_to_all | solution.py:127
  60.7 0.0 copy-done.2
  60.7 0.0 copy-start.8
  60.8 2.4 %tendency_kernel.1 = (bf16[512,256]{1,0:T(8,128)(2,1)S(1)}, f32[4,256,256]{2,1,0:T(8,128)}) custom-call(bf16[16,2,16,1024]{3,2,1,0:T(8,128)(2,1)S(1)} %bitcast.15, bf16[128,1152]{1,0:T(8,128)(2,1)S(1)} %copy-done.2, bf16[2048,512]{1,0:T(8,128)(2,1)S(1)} %get-tuple-element.9.refs_2_, bf16[2,384,256]{2,1,0:T(8,128)(2,1)S(1)} %get-tuple-element.10.refs_3_, ...), custom_call_target="tpu_custom_call" | custom-call | bytes 4882432 | tf_op jit(solution)/shard_map/tendency_kernel/pallas_call | solution.py:453
  63.2 12.9 %all_to_all.22 = bf16[32,16,256]{2,1,0:T(8,128)(2,1)S(1)} all-to-all(bf16[32,16,256]{2,1,0:T(8,128)(2,1)S(1)} %bitcast.21), channel_id=1, replica_groups=mesh['grp'=2,'hold'=2,'rest'=8,'lev'=1] {'grp','hold','rest'}, dimensions={0} | all-to-all | bytes 524288 | tf_op jit(solution)/shard_map/all_to_all | solution.py:127
  76.1 0.0 copy-done.4
  76.1 0.0 copy-done.6
  76.1 0.0 copy-done.7
  76.1 0.0 copy-done.8
  76.1 1.1 %analysis_kernel.1 = f32[2,64,256]{2,1,0:T(8,128)} custom-call(bf16[2,2,128,256]{3,2,1,0:T(8,128)(2,1)S(1)} %bitcast.18, bf16[256,256]{1,0:T(8,128)(2,1)S(1)} %copy-done.7, bf16[256,256]{1,0:T(8,128)(2,1)S(1)} %copy-done.6, bf16[2,64,128]{2,1,0:T(8,128)(2,1)S(1)} %copy-done.8, bf16[2,64,256]{2,1,0:T(8,128)(2,1)S(1)} %copy-done.4), custom_call_target="tpu_custom_call" | custom-call | bytes 622592 | tf_op jit(solution)/shard_map/analysis_kernel/pallas_call | solution.py:453
  (6 shorter events, 0.0 us)
Async XLA Ops:
  2.6 18.5 %all-to-all-start = ((bf16[32,16,256]{2,1,0:T(8,128)(2,1)}), bf16[32,16,256]{2,1,0:T(8,128)(2,1)S(1)}, u32[]{:S(2)}, u32[]{:S(2)}) async-start(bf16[32,16,256]{2,1,0:T(8,128)(2,1)} %bitcast.1), calls=%async_computation | async-start | bytes 524288 | tf_op jit(solution)/shard_map/all_to_all | solution.py:127
  10.0 11.1 %copy-start.5 = (bf16[384,256]{1,0:T(8,128)(2,1)S(1)}, bf16[384,256]{1,0:T(8,128)(2,1)}, u32[]{:S(2)}) copy-start(bf16[384,256]{1,0:T(8,128)(2,1)} %constant.23.clone.refs_1_) | copy-start | bytes 589828
  21.1 20.1 %copy-start = (f32[4,256,256]{2,1,0:T(8,128)S(1)}, f32[4,256,256]{2,1,0:T(8,128)}, u32[]{:S(2)}) copy-start(f32[4,256,256]{2,1,0:T(8,128)} %refs_2_.1) | copy-start | bytes 3145732
  21.1 20.1 %copy-start.1 = (f32[4,256,256]{2,1,0:T(8,128)S(1)}, f32[4,256,256]{2,1,0:T(8,128)}, u32[]{:S(2)}) copy-start(f32[4,256,256]{2,1,0:T(8,128)} %refs_4_.4) | copy-start | bytes 3145732
  21.1 20.1 %copy-start.3 = (f32[256,256]{1,0:T(8,128)S(1)}, f32[256,256]{1,0:T(8,128)}, u32[]{:S(2)}) copy-start(f32[256,256]{1,0:T(8,128)} %refs_3_.2) | copy-start | bytes 786436
  41.3 19.5 %copy-start.2 = (bf16[128,1152]{1,0:T(8,128)(2,1)S(1)}, bf16[128,1152]{1,0:T(8,128)(2,1)}, u32[]{:S(2)}) copy-start(bf16[128,1152]{1,0:T(8,128)(2,1)} %constant.24.clone.refs_1_) | copy-start | bytes 884740
  60.7 15.4 %copy-start.4 = (bf16[2,64,256]{2,1,0:T(8,128)(2,1)S(1)}, bf16[2,64,256]{2,1,0:T(8,128)(2,1)}, u32[]{:S(2)}) copy-start(bf16[2,64,256]{2,1,0:T(8,128)(2,1)} %refs_4_.5) | copy-start | bytes 196612
  60.7 15.4 %copy-start.6 = (bf16[256,256]{1,0:T(8,128)(2,1)S(1)}, bf16[256,256]{1,0:T(8,128)(2,1)}, u32[]{:S(2)}) copy-start(bf16[256,256]{1,0:T(8,128)(2,1)} %constant.32.refs_2_) | copy-start | bytes 393220
  60.7 15.4 %copy-start.7 = (bf16[256,256]{1,0:T(8,128)(2,1)S(1)}, bf16[256,256]{1,0:T(8,128)(2,1)}, u32[]{:S(2)}) copy-start(bf16[256,256]{1,0:T(8,128)(2,1)} %constant.26.clone.refs_1_) | copy-start | bytes 393220
  60.7 15.4 %copy-start.8 = (bf16[2,64,128]{2,1,0:T(8,128)(2,1)S(1)}, bf16[2,64,128]{2,1,0:T(8,128)(2,1)}, u32[]{:S(2)}) copy-start(bf16[2,64,128]{2,1,0:T(8,128)(2,1)} %refs_3_.3) | copy-start | bytes 98308
